TPU v7x, 32 devices: a whole 2x2x4 slice. The times are simulated.
32 devices in a mesh: dp: 16 (over z, y, core), tensor: 2 (over x).
Axes of the slice: x: 2, y: 2, z: 4, core: 2. Of those that a mesh axis runs over, the one named last changes fastest.
Arguments:
- latents_in: bfloat16 [16, 1024, 1152], P('dp', 'tensor'), may hold values from -6 to 6
- steps: int32 [16], P('dp'), may hold values from 0 to 999
- labels: int32 [16], P('dp'), may hold values from 0 to 999
- class_table: bfloat16 [1000, 1152], P(None, 'tensor'), may hold values from -6 to 6
- w_ada: bfloat16 [1152, 6912], P('tensor', 'dp'), may hold values from -0.1875 to 0.1875
- w_qkv: bfloat16 [3, 1152, 1152], P(None, 'dp', 'tensor'), may hold values from -0.1875 to 0.1875
- w_proj: bfloat16 [1152, 1152], P('tensor', 'dp'), may hold values from -3 to 3
- w_fc1: bfloat16 [1152, 4608], P('dp', 'tensor'), may hold values from -0.1875 to 0.1875
- w_fc2: bfloat16 [4608, 1152], P('tensor', 'dp'), may hold values from -0.09375 to 0.09375
- cotangent: bfloat16 [16, 1024, 1152], P('dp', 'tensor'), may hold values from -6 to 6
Outputs:
- block_out: bfloat16 [16, 1024, 1152], P('dp', 'tensor')
- grad_latents: float32 [16, 1024, 1152], P('dp', 'tensor')
- grad_class_table: float32 [1000, 1152], P(None, 'tensor')
- grad_w_ada: float32 [1152, 6912], P('tensor', 'dp')
- grad_w_qkv: float32 [3, 1152, 1152], P(None, 'dp', 'tensor')
- grad_w_proj: float32 [1152, 1152], P('tensor', 'dp')
- grad_w_fc1: float32 [1152, 4608], P('dp', 'tensor')
- grad_w_fc2: float32 [4608, 1152], P('tensor', 'dp')
All inputs are finite; a program needn't handle non-finite values.
Results may differ from a plain program's by a relative error of at most 0.02.
Values may be sent and summed in bfloat16 or wider, within the bound.
A program may use at most 192 MiB of HBM per device.

v0:
```python
import math

import jax
import jax.numpy as jnp
from jax import lax
from jax.sharding import PartitionSpec as P

D = 1152
H = 16


norm_epsilon = 1e-06
gelu_factor = 0.7978845608028654
gelu_cubic = 0.044715


def norm_rows(rows):
    average = jnp.mean(rows, axis=-1, keepdims=True)
    centred = rows - average
    variance = jnp.mean(centred * centred, axis=-1, keepdims=True)
    inv_std = lax.rsqrt(variance + norm_epsilon)
    return (centred * inv_std, inv_std)


def norm_back(grad_normed, normed, inv_std):
    first = jnp.mean(grad_normed, axis=-1, keepdims=True)
    second = jnp.mean(grad_normed * normed, axis=-1, keepdims=True)
    return inv_std * (grad_normed - first - normed * second)


def gelu_value(pre):
    inner = gelu_factor * (pre + gelu_cubic * pre * pre * pre)
    return 0.5 * pre * (1.0 + jnp.tanh(inner))


def gelu_slope(pre):
    tangent = jnp.tanh(gelu_factor * (pre + gelu_cubic * pre * pre * pre))
    return 0.5 * (1.0 + tangent) + 0.5 * pre * (1.0 - tangent * tangent) * gelu_factor * (
        1.0 + 3.0 * gelu_cubic * pre * pre
    )


def silu_value(value):
    return value * jax.nn.sigmoid(value)


def silu_slope(value):
    sigma = jax.nn.sigmoid(value)
    return sigma * (1.0 + value * (1.0 - sigma))


def time_columns(steps_float, columns, width):
    half = width // 2
    index = jnp.where(columns < half, columns, columns - half).astype(jnp.float32)
    freqs = jnp.exp(-math.log(10000.0) * index / half)
    angles = steps_float[:, None] * freqs[None, :]
    return jnp.where(columns[None, :] < half, jnp.cos(angles), jnp.sin(angles))


def attend(queries, keys, values, score_scale):
    tokens, heads, depth = queries.shape
    block = min(512, tokens)
    blocked = queries.reshape(tokens // block, block, heads, depth)

    def one_block(query_block):
        scores = (
            jnp.einsum("qhd,khd->hqk", query_block, keys, preferred_element_type=jnp.float32)
            * score_scale
        )
        largest = jnp.max(scores, axis=-1, keepdims=True)
        log_total = largest + jnp.log(jnp.sum(jnp.exp(scores - largest), axis=-1, keepdims=True))
        probs = jnp.exp(scores - log_total).astype(jnp.bfloat16)
        mixed = jnp.einsum("hqk,khd->qhd", probs, values, preferred_element_type=jnp.float32)
        return (mixed.astype(jnp.bfloat16), log_total[:, :, 0])

    mixed, log_totals = lax.map(one_block, blocked)
    return (mixed.reshape(tokens, heads, depth), log_totals)


def attend_back(queries, keys, values, mixed, grad_mixed, log_totals, score_scale):
    tokens, heads, depth = queries.shape
    block = min(512, tokens)
    shape = (tokens // block, block, heads, depth)
    zeros = jnp.zeros((tokens, heads, depth), jnp.float32)

    def one_block(carry, items):
        grad_keys, grad_values = carry
        query_block, mixed_block, grad_block, log_block = items
        scores = (
            jnp.einsum("qhd,khd->hqk", query_block, keys, preferred_element_type=jnp.float32)
            * score_scale
        )
        probs = jnp.exp(scores - log_block[:, :, None])
        grad_values = grad_values + jnp.einsum(
            "hqk,qhd->khd",
            probs.astype(jnp.bfloat16),
            grad_block,
            preferred_element_type=jnp.float32,
        )
        grad_probs = jnp.einsum(
            "qhd,khd->hqk", grad_block, values, preferred_element_type=jnp.float32
        )
        delta = jnp.sum(grad_block.astype(jnp.float32) * mixed_block.astype(jnp.float32), axis=-1)
        grad_scores = (
            probs * (grad_probs - jnp.swapaxes(delta, 0, 1)[:, :, None]) * score_scale
        ).astype(jnp.bfloat16)
        grad_queries = jnp.einsum(
            "hqk,khd->qhd", grad_scores, keys, preferred_element_type=jnp.float32
        )
        grad_keys = grad_keys + jnp.einsum(
            "hqk,qhd->khd", grad_scores, query_block, preferred_element_type=jnp.float32
        )
        return ((grad_keys, grad_values), grad_queries)

    items = (queries.reshape(shape), mixed.reshape(shape), grad_mixed.reshape(shape), log_totals)
    (grad_keys, grad_values), grad_queries = lax.scan(one_block, (zeros, zeros), items)
    return (grad_queries.reshape(tokens, heads, depth), grad_keys, grad_values)


def shards(latents_in, steps, labels, class_table, w_ada, w_qkv, w_proj, w_fc1, w_fc2, cotangent):
    rank = lax.axis_index("tensor")
    width = latents_in.shape[2]
    owned = class_table.shape[1]
    head_size = D // H
    heads_here = owned // head_size
    score_scale = head_size ** (-0.5)
    highest = lax.Precision.HIGHEST
    fetched = (
        lax.all_gather(w_qkv, "dp", axis=1, tiled=True),
        lax.all_gather(w_proj, "dp", axis=1, tiled=True),
        lax.all_gather(w_fc1, "dp", axis=0, tiled=True),
        lax.all_gather(w_fc2, "dp", axis=1, tiled=True),
        lax.all_gather(w_ada, "dp", axis=1, tiled=True),
    )
    qkv_full, proj_full, fc1_full, fc2_full, ada_full = fetched
    columns = rank * owned + jnp.arange(owned, dtype=jnp.int32)
    classes = jnp.arange(class_table.shape[0], dtype=jnp.int32)
    one_hot = (labels[:, None] == classes[None, :]).astype(jnp.bfloat16)
    cond = time_columns(steps.astype(jnp.float32), columns, D) + jnp.dot(
        one_hot, class_table, preferred_element_type=jnp.float32
    )
    cond_half = silu_value(cond).astype(jnp.bfloat16)
    mod_part = jnp.dot(cond_half, ada_full, preferred_element_type=jnp.float32)
    modulation = lax.psum(mod_part, "tensor").reshape(6, width)
    shift_a, scale_a, gate_a = (modulation[0], modulation[1], modulation[2])
    shift_m, scale_m, gate_m = (modulation[3], modulation[4], modulation[5])
    rows_in = latents_in[0].astype(jnp.float32)
    normed_a, inv_a = norm_rows(rows_in)
    mod_a = (normed_a * (1.0 + scale_a) + shift_a).astype(jnp.bfloat16)
    seq_a = lax.all_gather(mod_a, "tensor", axis=0, tiled=True)
    tokens = seq_a.shape[0]
    projected = jnp.einsum(
        "td,jdc->jtc", seq_a, qkv_full, preferred_element_type=jnp.float32
    ).astype(jnp.bfloat16)
    queries = projected[0].reshape(tokens, heads_here, head_size)
    keys = projected[1].reshape(tokens, heads_here, head_size)
    values = projected[2].reshape(tokens, heads_here, head_size)
    mixed, log_totals = attend(queries, keys, values, score_scale)
    mixed_flat = mixed.reshape(tokens, owned)
    attn_out = lax.psum_scatter(
        jnp.dot(mixed_flat, proj_full, preferred_element_type=jnp.float32).astype(jnp.bfloat16),
        "tensor",
        scatter_dimension=0,
        tiled=True,
    ).astype(jnp.float32)
    hidden = rows_in + gate_a * attn_out
    normed_m, inv_m = norm_rows(hidden)
    mod_m = (normed_m * (1.0 + scale_m) + shift_m).astype(jnp.bfloat16)
    piece = lax.all_gather(mod_m, "tensor", axis=0, tiled=True)
    pre_act = jnp.dot(piece, fc1_full, preferred_element_type=jnp.float32)
    acts = gelu_value(pre_act).astype(jnp.bfloat16)
    mlp_out = lax.psum_scatter(
        jnp.dot(acts, fc2_full, preferred_element_type=jnp.float32).astype(jnp.bfloat16),
        "tensor",
        scatter_dimension=0,
        tiled=True,
    ).astype(jnp.float32)
    block_out = (hidden + gate_m * mlp_out).astype(jnp.bfloat16)
    grad_out = cotangent[0].astype(jnp.float32)
    grad_gate_m = jnp.sum(grad_out * mlp_out, axis=0)
    grad_mlp = (grad_out * gate_m).astype(jnp.bfloat16)
    seq_grad_m = lax.all_gather(grad_mlp, "tensor", axis=0, tiled=True)
    grad_fc2 = jnp.einsum("tf,td->fd", acts, seq_grad_m, preferred_element_type=jnp.float32)
    grad_acts = jnp.einsum("td,fd->tf", seq_grad_m, fc2_full, preferred_element_type=jnp.float32)
    grad_pre = (grad_acts * gelu_slope(pre_act)).astype(jnp.bfloat16)
    grad_fc1 = jnp.einsum("td,tf->df", piece, grad_pre, preferred_element_type=jnp.float32)
    grad_mod_m = lax.psum_scatter(
        jnp.einsum("tf,df->td", grad_pre, fc1_full, preferred_element_type=jnp.float32).astype(
            jnp.bfloat16
        ),
        "tensor",
        scatter_dimension=0,
        tiled=True,
    ).astype(jnp.float32)
    grad_shift_m = jnp.sum(grad_mod_m, axis=0)
    grad_scale_m = jnp.sum(grad_mod_m * normed_m, axis=0)
    grad_hidden = grad_out + norm_back(grad_mod_m * (1.0 + scale_m), normed_m, inv_m)
    grad_gate_a = jnp.sum(grad_hidden * attn_out, axis=0)
    grad_attn = (grad_hidden * gate_a).astype(jnp.bfloat16)
    seq_grad_a = lax.all_gather(grad_attn, "tensor", axis=0, tiled=True)
    grad_proj = jnp.einsum("tc,td->cd", mixed_flat, seq_grad_a, preferred_element_type=jnp.float32)
    grad_mixed = jnp.einsum(
        "td,cd->tc", seq_grad_a, proj_full, preferred_element_type=jnp.float32
    ).astype(jnp.bfloat16)
    grad_queries, grad_keys, grad_values = attend_back(
        queries,
        keys,
        values,
        mixed,
        grad_mixed.reshape(tokens, heads_here, head_size),
        log_totals,
        score_scale,
    )
    grad_qkv = (
        jnp.stack([grad_queries, grad_keys, grad_values])
        .astype(jnp.bfloat16)
        .reshape(3, tokens, owned)
    )
    grad_w_qkv = jnp.einsum("td,jtc->jdc", seq_a, grad_qkv, preferred_element_type=jnp.float32)
    grad_mod_a = lax.psum_scatter(
        jnp.einsum("jtc,jdc->td", grad_qkv, qkv_full, preferred_element_type=jnp.float32).astype(
            jnp.bfloat16
        ),
        "tensor",
        scatter_dimension=0,
        tiled=True,
    ).astype(jnp.float32)
    grad_shift_a = jnp.sum(grad_mod_a, axis=0)
    grad_scale_a = jnp.sum(grad_mod_a * normed_a, axis=0)
    grad_input = grad_hidden + norm_back(grad_mod_a * (1.0 + scale_a), normed_a, inv_a)
    grad_mod_part = jnp.stack(
        [grad_shift_a, grad_scale_a, grad_gate_a, grad_shift_m, grad_scale_m, grad_gate_m]
    ).reshape(1, 6 * width)
    grad_modulation = lax.psum(grad_mod_part, "tensor")
    grad_ada = jnp.einsum(
        "lc,lm->cm", cond_half.astype(jnp.float32), grad_modulation, precision=highest
    )
    grad_cond = jnp.einsum(
        "lm,cm->lc", grad_modulation, ada_full.astype(jnp.float32), precision=highest
    ) * silu_slope(cond)
    grad_table_part = jnp.einsum(
        "ln,lc->nc", one_hot.astype(jnp.float32), grad_cond, precision=highest
    )
    grad_table = lax.psum(grad_table_part.astype(jnp.bfloat16), "dp").astype(jnp.float32)
    summed = (
        lax.psum_scatter(
            grad_ada.astype(jnp.bfloat16), "dp", scatter_dimension=1, tiled=True
        ).astype(jnp.float32),
        lax.psum_scatter(
            grad_w_qkv.astype(jnp.bfloat16), "dp", scatter_dimension=1, tiled=True
        ).astype(jnp.float32),
        lax.psum_scatter(
            grad_proj.astype(jnp.bfloat16), "dp", scatter_dimension=1, tiled=True
        ).astype(jnp.float32),
        lax.psum_scatter(
            grad_fc1.astype(jnp.bfloat16), "dp", scatter_dimension=0, tiled=True
        ).astype(jnp.float32),
        lax.psum_scatter(
            grad_fc2.astype(jnp.bfloat16), "dp", scatter_dimension=1, tiled=True
        ).astype(jnp.float32),
    )
    return (
        block_out[None],
        grad_input[None],
        grad_table,
        summed[0],
        summed[1],
        summed[2],
        summed[3],
        summed[4],
    )


def solution(mesh):
    return jax.shard_map(
        shards,
        mesh=mesh,
        in_specs=(
            P("dp", "tensor", None),
            P("dp"),
            P("dp"),
            P(None, "tensor"),
            P("tensor", "dp"),
            P(None, "dp", "tensor"),
            P("tensor", "dp"),
            P("dp", "tensor"),
            P("tensor", "dp"),
            P("dp", "tensor", None),
        ),
        out_specs=(
            P("dp", "tensor", None),
            P("dp", "tensor", None),
            P(None, "tensor"),
            P("tensor", "dp"),
            P(None, "dp", "tensor"),
            P("tensor", "dp"),
            P("dp", "tensor"),
            P("tensor", "dp"),
        ),
        check_vma=False,
    )
```

profile of v0, /device:TPU:0, one launch (start us, length us, event | category | flops | bytes accessed | tf_op | source)
XLA Modules:
  0.0 1207.0 jit_solution(4387460401471625936)
XLA Ops:
  12.5 77.7 %all-gather.10.cloned.1.call-done = bf16[576,6912]{0,1:T(8,128)(2,1)} async-done(((bf16[576,432]{0,1:T(8,128)(2,1)}), bf16[576,6912]{0,1:T(8,128)(2,1)}) %all-gather.10.cloned.1.call-update) | async-done | bytes 7962640 | tf_op jit(solution)/shard_map/all_gather | solution.py:133
  90.1 5.9 fusion.86
  96.0 8.3 psum.21
  107.2 35.4 %all-gather.14.cloned.1.call-done = bf16[3,1152,576]{2,1,0:T(8,128)(2,1)} async-done(((bf16[3,72,576]{2,1,0:T(8,128)(2,1)}), bf16[3,1152,576]{2,1,0:T(8,128)(2,1)}) %all-gather.14.cloned.1.call-update) | async-done | bytes 3981328 | tf_op jit(solution)/shard_map/all_gather | solution.py:129
  142.6 36.7 %all-gather.12.cloned.1.call-done = bf16[1024,1152]{1,0:T(8,128)(2,1)} async-done(((bf16[512,1152]{1,0:T(8,128)(2,1)}), bf16[1024,1152]{1,0:T(8,128)(2,1)}) %all-gather.12.cloned.1.call-update) | async-done | bytes 2359312 | tf_op jit(solution)/shard_map/all_gather | solution.py:150
  179.2 7.8 convert_bitcast_fusion
  188.9 4.2 reshape_reshape_squeeze.4
  195.6 21.8 %while.27 = (s32[]{:T(128)}, bf16[2,512,8,72]{1,3,2,0:T(8,128)(2,1)S(1)}, f32[2,8,512]{2,1,0:T(8,128)}, bf16[2,512,8,72]{1,3,2,0:T(8,128)(2,1)}, bf16[1024,8,72]...) while((s32[]{:T(128)}, bf16[2,512,8,72]{1,3,2,0:T(8,128)(2,1)S(1)}, ...), condition=%wide.region_6.7_spmd, body=%wide.region_3.6_spmd.sunk | while | flops 1241804800 | bytes 58982580 | solution.py:76
  220.5 5.4 convolution_convert_fusion.5
  226.5 33.8 %reduce-scatter.11.cloned.1.call-done = bf16[512,1152]{1,0:T(8,128)(2,1)} async-done(((bf16[1024,1152]{1,0:T(8,128)(2,1)}), bf16[512,1152]{1,0:T(8,128)(2,1)}) %reduce-scatter.11.cloned.1.call-update) | async-done | bytes 1179664 | tf_op jit(solution)/shard_map/reduce_scatter | solution.py:160
  268.5 50.2 %all-gather.20.cloned.1.call-done = bf16[1152,2304]{1,0:T(8,128)(2,1)} async-done(((bf16[72,2304]{1,0:T(8,128)(2,1)}), bf16[1152,2304]{1,0:T(8,128)(2,1)}) %all-gather.20.cloned.1.call-update) | async-done | bytes 5308432 | tf_op jit(solution)/shard_map/all_gather | solution.py:131
  318.7 36.8 %all-gather.18.cloned.1.call-done = bf16[1024,1152]{1,0:T(8,128)(2,1)} async-done(((bf16[512,1152]{1,0:T(8,128)(2,1)}), bf16[1024,1152]{1,0:T(8,128)(2,1)}) %all-gather.18.cloned.1.call-update) | async-done | bytes 2359312 | tf_op jit(solution)/shard_map/all_gather | solution.py:169
  355.5 11.8 fusion.87
  367.3 46.7 %all-gather.22.cloned.1.call-done = bf16[2304,1152]{0,1:T(8,128)(2,1)} async-done(((bf16[2304,72]{0,1:T(8,128)(2,1)}), bf16[2304,1152]{0,1:T(8,128)(2,1)}) %all-gather.22.cloned.1.call-update) | async-done | bytes 5308432 | tf_op jit(solution)/shard_map/all_gather | solution.py:132
  414.0 36.8 %all-gather.24.cloned.1.call-done = bf16[1024,1152]{1,0:T(8,128)(2,1)} async-done(((bf16[512,1152]{1,0:T(8,128)(2,1)}), bf16[1024,1152]{1,0:T(8,128)(2,1)}) %all-gather.24.cloned.1.call-update) | async-done | bytes 2359312 | tf_op jit(solution)/shard_map/all_gather | solution.py:182
  450.8 13.6 %fusion.38 = bf16[1024,2304]{1,0:T(8,128)(2,1)S(1)} fusion(f32[1024,2304]{1,0:T(8,128)} %fusion.87, bf16[1024,1152]{1,0:T(8,128)(2,1)} %all-gather.24.cloned.1.call-done, bf16[2304,1152]{0,1:T(8,128)(2,1)} %all-gather.22.cloned.1.call-done), kind=kOutput, calls=%fused_computation.52 | convolution fusion | flops 5480644608 | bytes 21823488 | tf_op jit(solution)/shard_map/td,fd->tf/dot_general | solution.py:184
  466.7 7.5 convolution_convert_fusion.3
  474.3 13.1 %convolution_convert_fusion.4 = bf16[1024,1152]{1,0:T(8,128)(2,1)} fusion(bf16[2304,1152]{0,1:T(8,128)(2,1)} %all-gather.22.cloned.1.call-done, f32[1024,2304]{1,0:T(8,128)} %fusion.87), kind=kOutput, calls=%fused_computation.58 | convolution fusion | flops 5458231296 | bytes 17104896 | tf_op jit(solution)/shard_map/dot_general | solution.py:173
  487.6 21.5 %reduce-scatter.15.cloned.1.call-done = bf16[512,1152]{1,0:T(8,128)(2,1)} async-done(((bf16[1024,1152]{1,0:T(8,128)(2,1)}), bf16[512,1152]{1,0:T(8,128)(2,1)}) %reduce-scatter.15.cloned.1.call-update) | async-done | bytes 1179664 | tf_op jit(solution)/shard_map/reduce_scatter | solution.py:187
  512.9 33.9 %reduce-scatter.13.cloned.1.call-done = bf16[512,1152]{1,0:T(8,128)(2,1)} async-done(((bf16[1024,1152]{1,0:T(8,128)(2,1)}), bf16[512,1152]{1,0:T(8,128)(2,1)}) %reduce-scatter.13.cloned.1.call-update) | async-done | bytes 1179664 | tf_op jit(solution)/shard_map/reduce_scatter | solution.py:172
  546.8 5.1 fusion.59
  554.6 36.1 %all-gather.26.cloned.1.call-done = bf16[1024,1152]{1,0:T(8,128)(2,1)} async-done(((bf16[512,1152]{1,0:T(8,128)(2,1)}), bf16[1024,1152]{1,0:T(8,128)(2,1)}) %all-gather.26.cloned.1.call-update) | async-done | bytes 2359312 | tf_op jit(solution)/shard_map/all_gather | solution.py:200
  590.7 3.8 convolution_convert_fusion.7
  595.6 65.6 %while.28 = (s32[]{:T(128)}, f32[1024,8,72]{0,2,1:T(8,128)}, f32[1024,8,72]{0,2,1:T(8,128)}, bf16[2,512,8,72]{1,3,2,0:T(8,128)(2,1)}, bf16[2,512,8,72]{1,3,2,0:T...) while((s32[]{:T(128)}, f32[1024,8,72]{0,2,1:T(8,128)}, ...), condition=%wide.region_16.17_spmd.clone, body=%wide.region_14.16_spmd.clone.sunk | while | flops 3061182464 | bytes 145719600 | solution.py:116
  597.7 3.8 fusion.148
  601.6 5.6 bitcast_add_fusion.5
  607.1 9.1 multiply_convert_fusion.10
  616.2 7.3 fusion.150
  623.5 4.3 bitcast_add_fusion.4
  629.9 3.8 fusion.148
  633.8 6.0 bitcast_add_fusion.5
  639.7 9.1 multiply_convert_fusion.10
  648.8 7.3 fusion.150
  656.1 5.1 bitcast_add_fusion.4
  669.3 7.1 bitcast_convert_fusion
  676.5 11.4 convolution_convert_fusion
  688.0 10.5 convolution_convert_fusion.1
  703.1 4.9 convolution_convert_fusion.6
  708.1 8.8 fusion.39
  716.9 11.7 copy.34
  731.8 7.2 psum.22
  739.0 5.9 convolution_reduce_fusion
  747.0 4.6 multiply_convert_fusion.1
  753.6 39.8 %reduce-scatter.23.cloned.1.call-done = bf16[2304,72]{0,1:T(8,128)(2,1)} async-done(((bf16[2304,1152]{0,1:T(8,128)(2,1)}), bf16[2304,72]{0,1:T(8,128)(2,1)}) %reduce-scatter.23.cloned.1.call-update) | async-done | bytes 331792 | tf_op jit(solution)/shard_map/reduce_scatter | solution.py:258
  795.3 79.2 %reduce-scatter.21.cloned.1.call-done = bf16[72,2304]{1,0:T(8,128)(2,1)} async-done(((bf16[1152,2304]{1,0:T(8,128)(2,1)}), bf16[72,2304]{1,0:T(8,128)(2,1)}) %reduce-scatter.21.cloned.1.call-update) | async-done | bytes 331792 | tf_op jit(solution)/shard_map/reduce_scatter | solution.py:255
  876.3 58.7 %reduce-scatter.25.cloned.1.call-done = bf16[576,72]{0,1:T(8,128)(2,1)} async-done(((bf16[576,1152]{0,1:T(8,128)(2,1)}), bf16[576,72]{0,1:T(8,128)(2,1)}) %reduce-scatter.25.cloned.1.call-update) | async-done | bytes 82960
  941.4 146.8 %all-reduce.5.cloned.1.call-done = (bf16[1000,576]{0,1:T(8,128)(2,1)}, bf16[3,1152,576]{2,0,1:T(4,128)(2,1)}) async-done(((bf16[1000,576]{0,1:T(8,128)(2,1)}, bf16[3,1152,576]{2,0,1:T(4,128)(2,1)}), (bf16[1000,576]{0,1:T(8,128)(2,1)}, bf16[3,1152,576]{2,0,1:T(4,128)(2,1)})) %all-reduce.5.cloned.1.call-update) | async-done | bytes 5133328 | tf_op jit(solution)/shard_map/psum | solution.py:244
  1091.9 105.9 %reduce-scatter.19.cloned.1.call-done = bf16[576,432]{0,1:T(8,128)(2,1)} async-done(((bf16[576,6912]{0,1:T(8,128)(2,1)}), bf16[576,432]{0,1:T(8,128)(2,1)}) %reduce-scatter.19.cloned.1.call-update) | async-done | bytes 497680 | tf_op jit(solution)/shard_map/reduce_scatter | solution.py:246
  (207 shorter events, 94.0 us)
Async XLA Ops:
  7.2 4.6 copy-start.5
  7.2 82.9 %all-gather.10.cloned.1.call-start = ((), (), s32[]{:S(2)}) async-start(), calls=%async_computation.8 | async-start | bytes 9400320 | tf_op jit(solution)/shard_map/all_gather | solution.py:133
  7.9 134.6 %all-gather.14.cloned.1.call-start = ((), (), s32[]{:S(2)}) async-start(), calls=%async_computation.10 | async-start | bytes 4700160 | tf_op jit(solution)/shard_map/all_gather | solution.py:129
  8.7 170.6 %all-gather.12.cloned.1.call-start = ((), (), s32[]{:S(2)}) async-start(), calls=%async_computation.9 | async-start | bytes 3538944 | tf_op jit(solution)/shard_map/all_gather | solution.py:150
  12.0 93.0 %copy-start.22 = (f32[512]{0:T(512)}, f32[512]{0:T(512)S(1)}, u32[]{:S(2)}) copy-start(f32[512]{0:T(512)S(1)} %broadcast_multiply_fusion.5) | copy-start | bytes 6148
  12.5 92.5 %copy-start.27 = (f32[512]{0:T(512)}, f32[512]{0:T(512)S(1)}, u32[]{:S(2)}) copy-start(f32[512]{0:T(512)S(1)} %add_rsqrt_fusion.1) | copy-start | bytes 6148
  106.5 114.0 %all-gather.16.cloned.1.call-start = ((), (), s32[]{:S(2)}) async-start(), calls=%async_computation.11 | async-start | bytes 1566720 | tf_op jit(solution)/shard_map/all_gather | solution.py:130
  107.1 153.2 %reduce-scatter.11.cloned.1.call-start = ((), (), s32[]{:S(2)}) async-start(), calls=%async_computation.12 | async-start | bytes 3538944 | tf_op jit(solution)/shard_map/reduce_scatter | solution.py:160
  199.2 3.6 copy-start.17
  199.2 3.6 copy-start.13
  202.8 3.7 copy-start.18
  210.1 3.6 copy-start.17
  210.1 3.6 copy-start.13
  213.7 3.7 copy-start.18
  225.9 92.8 %all-gather.20.cloned.1.call-start = ((), (), s32[]{:S(2)}) async-start(), calls=%async_computation.14 | async-start | bytes 5640192 | tf_op jit(solution)/shard_map/all_gather | solution.py:131
  226.5 129.0 %all-gather.18.cloned.1.call-start = ((), (), s32[]{:S(2)}) async-start(), calls=%async_computation.13 | async-start | bytes 3538944 | tf_op jit(solution)/shard_map/all_gather | solution.py:169
  265.1 148.9 %all-gather.22.cloned.1.call-start = ((), (), s32[]{:S(2)}) async-start(), calls=%async_computation.15 | async-start | bytes 5640192 | tf_op jit(solution)/shard_map/all_gather | solution.py:132
  265.8 185.0 %all-gather.24.cloned.1.call-start = ((), (), s32[]{:S(2)}) async-start(), calls=%async_computation.17 | async-start | bytes 3538944 | tf_op jit(solution)/shard_map/all_gather | solution.py:182
  268.4 240.7 %reduce-scatter.15.cloned.1.call-start = ((), (), s32[]{:S(2)}) async-start(), calls=%async_computation.18 | async-start | bytes 3538944 | tf_op jit(solution)/shard_map/reduce_scatter | solution.py:187
  450.8 15.9 %copy-start.38 = (bf16[1152,2304]{1,0:T(8,128)(2,1)S(1)}, bf16[1152,2304]{1,0:T(8,128)(2,1)}, u32[]{:S(2)}) copy-start(bf16[1152,2304]{1,0:T(8,128)(2,1)} %all-gather.20.cloned.1.call-done) | copy-start | bytes 15925252
  474.2 72.6 %reduce-scatter.13.cloned.1.call-start = ((), (), s32[]{:S(2)}) async-start(), calls=%async_computation.16 | async-start | bytes 3538944 | tf_op jit(solution)/shard_map/reduce_scatter | solution.py:172
  487.4 103.3 %all-gather.26.cloned.1.call-start = ((), (), s32[]{:S(2)}) async-start(), calls=%async_computation.19 | async-start | bytes 3538944 | tf_op jit(solution)/shard_map/all_gather | solution.py:200
  554.5 174.1 %reduce-scatter.17.cloned.1.call-start = ((), (), s32[]{:S(2)}) async-start(), calls=%async_computation.20 | async-start | bytes 3538944 | tf_op jit(solution)/shard_map/reduce_scatter | solution.py:220
  616.2 7.3 copy-start.2
  623.5 4.3 copy-start.4
  623.5 4.3 copy-start.8
  648.8 7.3 copy-start.2
  656.1 5.1 copy-start.4
  656.1 5.1 copy-start.8
  665.0 4.3 copy-start.16
  665.0 4.3 copy-start.39
  676.4 117.0 %reduce-scatter.23.cloned.1.call-start = ((), (), s32[]{:S(2)}) async-start(), calls=%async_computation.23 | async-start | bytes 5640192 | tf_op jit(solution)/shard_map/reduce_scatter | solution.py:258
  687.9 186.5 %reduce-scatter.21.cloned.1.call-start = ((), (), s32[]{:S(2)}) async-start(), calls=%async_computation.22 | async-start | bytes 5640192 | tf_op jit(solution)/shard_map/reduce_scatter | solution.py:255
  698.5 4.0 copy-start.30
  698.5 4.6 copy-start.15
  698.5 236.5 %reduce-scatter.25.cloned.1.call-start = ((), (), s32[]{:S(2)}) async-start(), calls=%async_computation.24 | async-start | bytes 1566720
  708.0 380.2 %all-reduce.5.cloned.1.call-start = ((), (), s32[]{:S(2)}) async-start(), calls=%async_computation.25 | async-start | bytes 14155776 | tf_op jit(solution)/shard_map/psum | solution.py:244
  716.9 11.8 copy-start.6
  716.9 11.8 copy-start.20
  716.9 11.8 copy-start.23
  716.9 11.8 copy-start.28
  728.6 3.2 copy-start.34
  728.6 3.2 copy-start.35
  739.0 6.0 copy-start.25
  739.0 6.0 copy-start.36
  746.3 451.5 %reduce-scatter.19.cloned.1.call-start = ((), (), s32[]{:S(2)}) async-start(), calls=%async_computation.21 | async-start | bytes 9400320 | tf_op jit(solution)/shard_map/reduce_scatter | solution.py:246
  751.5 186.4 %copy-start.11 = (f32[512,1152]{1,0:T(8,128)S(1)}, f32[512,1152]{1,0:T(8,128)}, u32[]{:S(2)}) copy-start(f32[512,1152]{1,0:T(8,128)} %copy-done.10) | copy-start | bytes 7077892
  1090.2 109.7 %copy-start.1 = (bf16[1000,576]{0,1:T(8,128)(2,1)S(1)}, bf16[1000,576]{0,1:T(8,128)(2,1)}, u32[]{:S(2)}) copy-start(bf16[1000,576]{0,1:T(8,128)(2,1)} %param.17) | copy-start | bytes 3456004
  (19 other events, 36.1 us)
Sparse Core Ops, SparseCore 0:
  10.2 79.8 all-gather.9
  92.3 50.1 all-gather.13
  144.7 34.5 all-gather.11
  181.3 39.1 all-gather.15
  226.0 34.2 reduce-scatter.10
  262.3 56.3 all-gather.19
  320.8 34.6 all-gather.17
  357.7 56.3 all-gather.21
  416.1 34.6 all-gather.23
  474.3 34.7 reduce-scatter.14
  512.0 34.7 reduce-scatter.12
  554.6 36.0 all-gather.25
  676.6 34.7 reduce-scatter.16
  715.3 78.1 reduce-scatter.22
  797.3 77.0 reduce-scatter.20
  878.0 56.8 reduce-scatter.24
  938.6 149.5 all-reduce.4
  1092.2 105.5 reduce-scatter.18
where the time goes:
time: 1210 us
  waiting for transfers between devices  880 us (73%)
  matrix products  194 us (16%)
  other arithmetic  58.7 us (5%)
  local copies, waits for them, and re-layouts  40.7 us (3%)
  between operations  16.9 us (1%)
  blocking collectives  15.5 us (1%)
    psum x1, waiting for transfers between devices, shards(): lax.psum(grad_table_part.astype(jnp.bfloat16), 'dp').astype(jnp.float32)  147 us
    reduce_scatter x1, waiting for transfers between devices, shards(): lax.psum_scatter(grad_ada.astype(jnp.bfloat16), 'dp', scatter_dimension=1...  106 us
    reduce_scatter x1, waiting for transfers between devices, shards(): lax.psum_scatter(grad_fc1.astype(jnp.bfloat16), 'dp', scatter_dimension=0...  79.2 us
    all_gather x1, waiting for transfers between devices, shards(): lax.all_gather(w_ada, 'dp', axis=1, tiled=True)  77.7 us
    unnamed x19, waiting for transfers between devices  62 us
    all_gather x1, waiting for transfers between devices, shards(): lax.all_gather(w_fc1, 'dp', axis=0, tiled=True)  50.2 us
    all_gather x1, waiting for transfers between devices, shards(): lax.all_gather(w_fc2, 'dp', axis=1, tiled=True)  46.7 us
    reduce_scatter x1, waiting for transfers between devices, shards(): lax.psum_scatter(grad_fc2.astype(jnp.bfloat16), 'dp', scatter_dimension=1...  39.8 us
  transfers between devices with their start and end apart: 18, of which 17 were waited for; matrix products, arithmetic and copies ran while one was open for 14% of the time, Pallas kernels for 0%

commit v1 on v0

v1 whole, which is shorter than its diff:
```python
import functools
import math

import jax
import jax.numpy as jnp
from jax import lax
from jax.sharding import PartitionSpec as P

D = 1152
H = 16


norm_epsilon = 1e-06
gelu_factor = 0.7978845608028654
gelu_cubic = 0.044715


def norm_rows(rows):
    average = jnp.mean(rows, axis=-1, keepdims=True)
    centred = rows - average
    variance = jnp.mean(centred * centred, axis=-1, keepdims=True)
    inv_std = lax.rsqrt(variance + norm_epsilon)
    return (centred * inv_std, inv_std)


def norm_back(grad_normed, normed, inv_std):
    first = jnp.mean(grad_normed, axis=-1, keepdims=True)
    second = jnp.mean(grad_normed * normed, axis=-1, keepdims=True)
    return inv_std * (grad_normed - first - normed * second)


def gelu_value(pre):
    inner = gelu_factor * (pre + gelu_cubic * pre * pre * pre)
    return 0.5 * pre * (1.0 + jnp.tanh(inner))


def gelu_slope(pre):
    tangent = jnp.tanh(gelu_factor * (pre + gelu_cubic * pre * pre * pre))
    return 0.5 * (1.0 + tangent) + 0.5 * pre * (1.0 - tangent * tangent) * gelu_factor * (
        1.0 + 3.0 * gelu_cubic * pre * pre
    )


def silu_value(value):
    return value * jax.nn.sigmoid(value)


def silu_slope(value):
    sigma = jax.nn.sigmoid(value)
    return sigma * (1.0 + value * (1.0 - sigma))


def time_columns(steps_float, columns, width):
    half = width // 2
    index = jnp.where(columns < half, columns, columns - half).astype(jnp.float32)
    freqs = jnp.exp(-math.log(10000.0) * index / half)
    angles = steps_float[:, None] * freqs[None, :]
    return jnp.where(columns[None, :] < half, jnp.cos(angles), jnp.sin(angles))


def attend(queries, keys, values, score_scale):
    scores = (
        jnp.einsum("qhd,khd->hqk", queries, keys, preferred_element_type=jnp.float32) * score_scale
    )
    largest = jnp.max(scores, axis=-1, keepdims=True)
    log_total = largest + jnp.log(jnp.sum(jnp.exp(scores - largest), axis=-1, keepdims=True))
    probs = jnp.exp(scores - log_total).astype(jnp.bfloat16)
    mixed = jnp.einsum("hqk,khd->qhd", probs, values, preferred_element_type=jnp.float32)
    return (mixed.astype(jnp.bfloat16), log_total[:, :, 0])


def attend_back(queries, keys, values, mixed, grad_mixed, log_totals, score_scale):
    scores = (
        jnp.einsum("qhd,khd->hqk", queries, keys, preferred_element_type=jnp.float32) * score_scale
    )
    probs = jnp.exp(scores - log_totals[:, :, None])
    grad_values = jnp.einsum(
        "hqk,qhd->khd", probs.astype(jnp.bfloat16), grad_mixed, preferred_element_type=jnp.float32
    )
    grad_probs = jnp.einsum("qhd,khd->hqk", grad_mixed, values, preferred_element_type=jnp.float32)
    delta = jnp.sum(grad_mixed.astype(jnp.float32) * mixed.astype(jnp.float32), axis=-1)
    grad_scores = (
        probs * (grad_probs - jnp.swapaxes(delta, 0, 1)[:, :, None]) * score_scale
    ).astype(jnp.bfloat16)
    grad_queries = jnp.einsum("hqk,khd->qhd", grad_scores, keys, preferred_element_type=jnp.float32)
    grad_keys = jnp.einsum("hqk,qhd->khd", grad_scores, queries, preferred_element_type=jnp.float32)
    return (grad_queries, grad_keys, grad_values)


def from_rank(value, ranks, step):
    return lax.ppermute(value, "tensor", [(i, (i - step) % ranks) for i in range(ranks)])


def fetch_rest(rows, ranks):
    got = [from_rank(rows, ranks, step) for step in range(1, ranks)]
    return got[0] if ranks == 2 else jnp.concatenate(got, axis=0)


def return_rest(partial, ranks):
    size = partial.shape[0] // (ranks - 1)
    total = None
    for step in range(1, ranks):
        part = partial[(step - 1) * size : step * size].astype(jnp.bfloat16)
        part = from_rank(part, ranks, ranks - step).astype(jnp.float32)
        total = part if total is None else total + part
    return total


def sum_ranks(value, ranks):
    total = value
    for step in range(1, ranks):
        total = total + from_rank(value, ranks, step)
    return total


def dot(spec, left, right):
    return jnp.einsum(spec, left, right, preferred_element_type=jnp.float32)


def join(own, rest):
    return jnp.concatenate([own, rest], axis=0)


def shards(
    ranks, latents_in, steps, labels, class_table, w_ada, w_qkv, w_proj, w_fc1, w_fc2, cotangent
):
    half = jnp.bfloat16
    rank = lax.axis_index("tensor")
    width = latents_in.shape[2]
    mine = latents_in.shape[1]
    owned = class_table.shape[1]
    head_size = D // H
    heads_here = owned // head_size
    score_scale = head_size ** (-0.5)
    highest = lax.Precision.HIGHEST
    marks = lax.all_gather(jnp.stack([steps, labels], axis=1), "dp", axis=0, tiled=True)
    all_steps, all_labels = marks[:, 0], marks[:, 1]
    attn_w = lax.all_gather(
        jnp.concatenate([w_qkv[0], w_qkv[1], w_qkv[2], w_proj.T], axis=1),
        "dp",
        axis=0,
        tiled=True,
    )
    mlp_w = lax.all_gather(jnp.concatenate([w_fc1, w_fc2.T], axis=1), "dp", axis=0, tiled=True)
    qkv_full, proj_t = attn_w[:, : 3 * owned], attn_w[:, 3 * owned :]
    fc1_full, fc2_t = mlp_w[:, : w_fc1.shape[1]], mlp_w[:, w_fc1.shape[1] :]
    columns = rank * owned + jnp.arange(owned, dtype=jnp.int32)
    classes = jnp.arange(class_table.shape[0], dtype=jnp.int32)
    one_hot = (all_labels[:, None] == classes[None, :]).astype(half)
    cond = time_columns(all_steps.astype(jnp.float32), columns, D) + jnp.dot(
        one_hot, class_table, preferred_element_type=jnp.float32
    )
    cond_half = silu_value(cond).astype(half)
    mod_part = jnp.dot(cond_half, w_ada, preferred_element_type=jnp.float32)
    modulation = lax.all_to_all(sum_ranks(mod_part, ranks), "dp", 0, 0, tiled=True)
    modulation = modulation.reshape(6, width)
    shift_a, scale_a, gate_a = (modulation[0], modulation[1], modulation[2])
    shift_m, scale_m, gate_m = (modulation[3], modulation[4], modulation[5])
    rows_in = latents_in[0].astype(jnp.float32)
    normed_a, inv_a = norm_rows(rows_in)
    mod_a = (normed_a * (1.0 + scale_a) + shift_a).astype(half)
    rest_a = fetch_rest(mod_a, ranks)
    grad_out = cotangent[0].astype(jnp.float32)
    grad_mlp = (grad_out * gate_m).astype(half)
    rest_grad_m = fetch_rest(grad_mlp, ranks)
    qkv_own = dot("td,dc->tc", mod_a, qkv_full).astype(half)
    qkv_rest = dot("td,dc->tc", rest_a, qkv_full).astype(half)
    projected = join(qkv_own, qkv_rest)
    tokens = projected.shape[0]
    queries = projected[:, :owned].reshape(tokens, heads_here, head_size)
    keys = projected[:, owned : 2 * owned].reshape(tokens, heads_here, head_size)
    values = projected[:, 2 * owned :].reshape(tokens, heads_here, head_size)
    mixed_rest, log_rest = attend(queries[mine:], keys, values, score_scale)
    mixed_rest_flat = mixed_rest.reshape(tokens - mine, owned)
    attn_away = return_rest(dot("tc,dc->td", mixed_rest_flat, proj_t), ranks)
    mixed_own, log_own = attend(queries[:mine], keys, values, score_scale)
    mixed_own_flat = mixed_own.reshape(mine, owned)
    attn_out = dot("tc,dc->td", mixed_own_flat, proj_t) + attn_away
    hidden = rows_in + gate_a * attn_out
    normed_m, inv_m = norm_rows(hidden)
    mod_m = (normed_m * (1.0 + scale_m) + shift_m).astype(half)
    rest_m = fetch_rest(mod_m, ranks)
    pre_own = dot("td,df->tf", mod_m, fc1_full)
    acts_own = gelu_value(pre_own).astype(half)
    pre_rest = dot("td,df->tf", rest_m, fc1_full)
    acts_rest = gelu_value(pre_rest).astype(half)
    mlp_away = return_rest(dot("tf,df->td", acts_rest, fc2_t), ranks)
    grad_pre_rest = (dot("td,df->tf", rest_grad_m, fc2_t) * gelu_slope(pre_rest)).astype(half)
    grad_mod_away = return_rest(dot("tf,df->td", grad_pre_rest, fc1_full), ranks)
    mlp_out = dot("tf,df->td", acts_own, fc2_t) + mlp_away
    block_out = (hidden + gate_m * mlp_out).astype(half)
    grad_gate_m = jnp.sum(grad_out * mlp_out, axis=0)
    grad_pre_own = (dot("td,df->tf", grad_mlp, fc2_t) * gelu_slope(pre_own)).astype(half)
    grad_mod_m = dot("tf,df->td", grad_pre_own, fc1_full) + grad_mod_away
    grad_fc2_t = dot("td,tf->df", join(grad_mlp, rest_grad_m), join(acts_own, acts_rest))
    grad_fc1 = dot("td,tf->df", join(mod_m, rest_m), join(grad_pre_own, grad_pre_rest))
    mlp_w_part = jnp.concatenate([grad_fc1.astype(half), grad_fc2_t.astype(half)], axis=1)
    mlp_w_part, grad_mod_m = lax.optimization_barrier((mlp_w_part, grad_mod_m))
    grad_mlp_w = lax.psum_scatter(
        mlp_w_part,
        "dp",
        scatter_dimension=0,
        tiled=True,
    ).astype(jnp.float32)
    grad_shift_m = jnp.sum(grad_mod_m, axis=0)
    grad_scale_m = jnp.sum(grad_mod_m * normed_m, axis=0)
    grad_hidden = grad_out + norm_back(grad_mod_m * (1.0 + scale_m), normed_m, inv_m)
    grad_gate_a = jnp.sum(grad_hidden * attn_out, axis=0)
    grad_attn = (grad_hidden * gate_a).astype(half)
    rest_grad_a = fetch_rest(grad_attn, ranks)
    grad_mixed_own = dot("td,dc->tc", grad_attn, proj_t).astype(half)
    grad_mixed_rest = dot("td,dc->tc", rest_grad_a, proj_t).astype(half)
    mixed_flat = join(mixed_own_flat, mixed_rest_flat)
    grad_proj_t = dot("td,tc->dc", join(grad_attn, rest_grad_a), mixed_flat)
    grad_mixed = join(grad_mixed_own, grad_mixed_rest)
    grads = attend_back(
        queries,
        keys,
        values,
        mixed_flat.reshape(tokens, heads_here, head_size),
        grad_mixed.reshape(tokens, heads_here, head_size),
        jnp.concatenate([log_own, log_rest], axis=1),
        score_scale,
    )
    grad_qkv = jnp.concatenate([g.astype(half).reshape(tokens, owned) for g in grads], axis=1)
    grad_a_away = return_rest(dot("tc,dc->td", grad_qkv[mine:], qkv_full), ranks)
    grad_w_qkv = dot("td,tc->dc", join(mod_a, rest_a), grad_qkv)
    attn_w_part = jnp.concatenate([grad_w_qkv.astype(half), grad_proj_t.astype(half)], axis=1)
    attn_w_part, grad_mlp_w = lax.optimization_barrier((attn_w_part, grad_mlp_w))
    grad_attn_w = lax.psum_scatter(
        attn_w_part,
        "dp",
        scatter_dimension=0,
        tiled=True,
    ).astype(jnp.float32)
    grad_mod_a = dot("tc,dc->td", grad_qkv[:mine], qkv_full) + grad_a_away
    grad_shift_a = jnp.sum(grad_mod_a, axis=0)
    grad_scale_a = jnp.sum(grad_mod_a * normed_a, axis=0)
    grad_input = grad_hidden + norm_back(grad_mod_a * (1.0 + scale_a), normed_a, inv_a)
    grad_mod_part = jnp.stack(
        [grad_shift_a, grad_scale_a, grad_gate_a, grad_shift_m, grad_scale_m, grad_gate_m]
    ).reshape(all_steps.shape[0], w_ada.shape[1])
    grad_modulation = lax.all_to_all(sum_ranks(grad_mod_part, ranks), "dp", 0, 0, tiled=True)
    grad_ada = jnp.einsum(
        "lc,lm->cm", cond_half.astype(jnp.float32), grad_modulation, precision=highest
    )
    grad_cond = lax.psum(
        jnp.einsum("lm,cm->lc", grad_modulation, w_ada.astype(jnp.float32), precision=highest),
        "dp",
    ) * silu_slope(cond)
    grad_table = jnp.einsum("ln,lc->nc", one_hot.astype(jnp.float32), grad_cond, precision=highest)
    return (
        block_out[None],
        grad_input[None],
        grad_table,
        grad_ada,
        jnp.stack([grad_attn_w[:, j * owned : (j + 1) * owned] for j in range(3)]),
        grad_attn_w[:, 3 * owned :].T,
        grad_mlp_w[:, : w_fc1.shape[1]],
        grad_mlp_w[:, w_fc1.shape[1] :].T,
    )


def solution(mesh):
    return jax.shard_map(
        functools.partial(shards, mesh.shape["tensor"]),
        mesh=mesh,
        in_specs=(
            P("dp", "tensor", None),
            P("dp"),
            P("dp"),
            P(None, "tensor"),
            P("tensor", "dp"),
            P(None, "dp", "tensor"),
            P("tensor", "dp"),
            P("dp", "tensor"),
            P("tensor", "dp"),
            P("dp", "tensor", None),
        ),
        out_specs=(
            P("dp", "tensor", None),
            P("dp", "tensor", None),
            P(None, "tensor"),
            P("tensor", "dp"),
            P(None, "dp", "tensor"),
            P("tensor", "dp"),
            P("dp", "tensor"),
            P("tensor", "dp"),
        ),
        check_vma=False,
    )
```

time: 1210 us -> 534 us (0.44)
  waiting for transfers between devices: 880 us -> 137 us
  blocking collectives: 15.5 us -> 83.1 us
  starting transfers between devices: 1.29 us -> 23.1 us
  other arithmetic: 58.7 us -> 41.1 us
  local copies, waits for them, and re-layouts: 40.7 us -> 27.7 us
    all_gather x9 -> x2, waiting for transfers between devices: 357 us -> 0.01 us  [the longest x1 0.01 us: shards(): lax.all_gather(jnp.concatenate([w_qkv[0], w_qkv[1], w_qkv[2], w_proj.T],...]
    reduce_scatter x7 -> x1, waiting for transfers between devices: 314 us -> 0.01 us  [shards(): lax.psum_scatter(mlp_w_part, 'dp', scatter_dimension=0, tiled=True)]
    psum x1 -> x0, waiting for transfers between devices: 147 us -> none  [shards(): lax.psum(grad_table_part.astype(jnp.bfloat16), 'dp').astype(jnp.float32)]
    ppermute x0 -> x10, waiting for transfers between devices: none -> 127 us  [from_rank(): lax.ppermute(value, 'tensor', [(i, (i - step) % ranks) for i in range(ran...]
    unnamed x19 -> x5, waiting for transfers between devices: 62 us -> 0.07 us
    psum x2 -> x1, blocking collectives: 15.5 us -> 59.8 us  [shards(): lax.psum(jnp.einsum('lm,cm->lc', grad_modulation, w_ada.astype(jnp.float3...]
    all_gather x0 -> x1, blocking collectives: none -> 23.3 us  [shards(): lax.all_gather(jnp.stack([steps, labels], axis=1), 'dp', axis=0, tiled=True)]
    convert_element_type x12 -> x6, other arithmetic: 22.9 us -> 4.65 us  [the longest x1 2.23 us: shards(): grad_mlp_w = lax.psum_scatter(mlp_w_part, 'dp', scatter_dimension=0, tile...]
  transfers between devices with their start and end apart: 18 -> 16, of which waited for: 17 -> 11; matrix products, arithmetic and copies ran while one was open for 14% -> 43% of each run, Pallas kernels for 0% -> 0%
where the time goes in v1:
time: 534 us; the launch traced here: 526 us
  matrix products  198 us (37%)
  waiting for transfers between devices  137 us (26%)
  blocking collectives  83.1 us (16%)
  other arithmetic  41.1 us (8%)
  local copies, waits for them, and re-layouts  27.7 us (5%)
  starting transfers between devices  23.1 us (4%)
  between operations  16.3 us (3%)
    ppermute x10, waiting for transfers between devices, from_rank(): lax.ppermute(value, 'tensor', [(i, (i - step) % ranks) for i in range(ran...  127 us
    dot_general x20, matrix products, dot(): return jnp.einsum(spec, left, right, preferred_element_type=jnp.float32)  110 us
    psum x1, blocking collectives, shards(): lax.psum(jnp.einsum('lm,cm->lc', grad_modulation, w_ada.astype(jnp.float3...  59.8 us
    all_gather x1, blocking collectives, shards(): lax.all_gather(jnp.stack([steps, labels], axis=1), 'dp', axis=0, tiled=True)  23.3 us
    dot_general x1, matrix products, attend_back(): jnp.einsum('qhd,khd->hqk', grad_mixed, values, preferred_element_type=jnp...  19.7 us
    unnamed x138, local copies, waits for them, and re-layouts  15.4 us
    dot_general x1, matrix products, attend_back(): jnp.einsum('qhd,khd->hqk', queries, keys, preferred_element_type=jnp.floa...  13.3 us
    dot_general x1, matrix products, attend_back(): jnp.einsum('hqk,qhd->khd', probs.astype(jnp.bfloat16), grad_mixed, prefer...  13.2 us
  transfers between devices with their start and end apart: 16, of which 11 were waited for; matrix products, arithmetic and copies ran while one was open for 43% of the time, Pallas kernels for 0%

profile of v1, /device:TPU:0, one launch (start us, length us, event | category | flops | bytes accessed | tf_op | source)
XLA Modules:
  0.0 526.4 jit_solution(4783316110772384095)
XLA Ops:
  13.7 23.3 %all-gather = s32[16,1,2]{2,1,0:T(1,128)S(1)} all-gather(s32[1,1,2]{2,1,0:T(1,128)S(1)} %add_bitcast_fusion.1), channel_id=1, replica_groups=mesh['dp'=16,'tensor'=2] {'dp'}, dimensions={0}, use_global_device_ids=true | all-gather | bytes 136 | tf_op jit(solution)/shard_map/all_gather | solution.py:136
  42.8 3.5 all-to-all-start
  46.3 7.2 %all-to-all-done = f32[16,1,432]{2,1,0:T(1,128)S(1)} async-done(((f32[16,1,432]{2,1,0:T(1,128)}), f32[16,1,432]{2,1,0:T(1,128)S(1)}, u32[]{:S(2)}, u32[]{:S(2)}) %all-to-all-start) | async-done | bytes 27680 | tf_op jit(solution)/shard_map/all_to_all | solution.py:155
  56.5 25.9 %collective-permute-done.1 = bf16[512,1152]{1,0:T(8,128)(2,1)S(1)} collective-permute-done((bf16[512,1152]{1,0:T(8,128)(2,1)S(1)}, bf16[512,1152]{1,0:T(8,128)(2,1)S(1)}, u32[]{:S(2)}, u32[]{:S(2)}) %collective-permute-start.1) | collective-permute-done | bytes 1179680 | tf_op jit(solution)/shard_map/ppermute | solution.py:91
  82.3 5.1 convolution_convert_fusion.6
  87.6 2.5 convolution_convert_fusion.7
  90.1 3.3 pad_maximum_fusion.3
  95.9 3.5 exponential_reduce_fusion
  99.5 3.7 fusion.88
  103.2 3.2 convolution_convert_fusion.5
  108.0 2.5 multiply_reduce_fusion.1
  110.5 3.5 exponential_reduce_fusion.1
  114.1 4.1 fusion.89
  118.2 14.8 %collective-permute-done.2 = bf16[512,1152]{1,0:T(8,128)(2,1)S(1)} collective-permute-done((bf16[512,1152]{1,0:T(8,128)(2,1)S(1)}, bf16[512,1152]{1,0:T(8,128)(2,1)S(1)}, u32[]{:S(2)}, u32[]{:S(2)}) %collective-permute-start.2) | collective-permute-done | bytes 1179680 | tf_op jit(solution)/shard_map/ppermute | solution.py:91
  133.0 4.9 fusion.132
  142.5 25.7 %collective-permute-done.3 = bf16[512,1152]{1,0:T(8,128)(2,1)} collective-permute-done((bf16[512,1152]{1,0:T(8,128)(2,1)S(1)}, bf16[512,1152]{1,0:T(8,128)(2,1)}, u32[]{:S(2)}, u32[]{:S(2)}) %collective-permute-start.3) | collective-permute-done | bytes 1179680 | tf_op jit(solution)/shard_map/ppermute | solution.py:91
  168.1 8.4 %multiply_convert_fusion.1 = (bf16[512,2304]{1,0:T(8,128)(2,1)}, f32[512,2304]{1,0:T(8,128)S(1)}) fusion(bf16[512,1152]{1,0:T(8,128)(2,1)} %collective-permute-done.3, bf16[1152,4608]{1,0:T(8,128)(2,1)} %all-gather.6.cloned.1.call-done), kind=kOutput, calls=%fused_computation.39 | convolution fusion | flops 2728525824 | bytes 13565952 | tf_op jit(solution)/shard_map/td,df->tf/dot_general | solution.py:117
  176.5 13.8 %collective-permute-done.5 = bf16[512,1152]{1,0:T(8,128)(2,1)} collective-permute-done((bf16[512,1152]{1,0:T(8,128)(2,1)}, bf16[512,1152]{1,0:T(8,128)(2,1)}, u32[]{:S(2)}, u32[]{:S(2)}) %collective-permute-start.5) | collective-permute-done | bytes 1179680 | tf_op jit(solution)/shard_map/ppermute | solution.py:91
  190.4 6.6 %fusion.22 = bf16[512,2304]{1,0:T(8,128)(2,1)S(1)} fusion(f32[512,2304]{1,0:T(8,128)S(1)} %get-tuple-element.76, bf16[512,1152]{1,0:T(8,128)(2,1)} %collective-permute-done.5, bf16[1152,4608]{1,0:T(8,128)(2,1)S(1)} %copy-done.56), kind=kOutput, calls=%fused_computation.42 | convolution fusion | flops 2740322304 | bytes 13565952 | tf_op jit(solution)/shard_map/td,df->tf/dot_general | solution.py:117
  197.0 4.2 fusion.37
  202.7 3.8 multiply_convert_fusion.2
  206.6 7.4 %fusion.21 = bf16[512,2304]{1,0:T(8,128)(2,1)S(1)} fusion(f32[512,2304]{1,0:T(8,128)S(1)} %get-tuple-element.74, bf16[512,1152]{1,0:T(8,128)(2,1)} %fusion.65, bf16[1152,4608]{1,0:T(8,128)(2,1)S(1)} %copy-done.56), kind=kOutput, calls=%fused_computation.41 | convolution fusion | flops 2740322304 | bytes 13565952 | tf_op jit(solution)/shard_map/td,df->tf/dot_general | solution.py:117
  214.0 9.1 %convolution_convert_fusion.1 = bf16[1152,2304]{1,0:T(8,128)(2,1)S(1)} fusion(bf16[512,2304]{1,0:T(8,128)(2,1)} %copy-done.62, bf16[512,2304]{1,0:T(8,128)(2,1)S(1)} %fusion.21, bf16[512,1152]{1,0:T(8,128)(2,1)} %collective-permute-done.3, bf16[512,1152]{1,0:T(8,128)(2,1)S(1)} %copy-done.28), kind=kOutput, calls=%fused_computation.11 | convolution fusion | flops 5452627968 | bytes 12386304 | tf_op jit(solution)/shard_map/td,tf->df/dot_general | solution.py:117
  223.2 7.9 %convolution_convert_fusion = bf16[1152,2304]{1,0:T(8,128)(2,1)S(1)} fusion(bf16[512,2304]{1,0:T(8,128)(2,1)S(1)} %copy-done.61, bf16[512,2304]{1,0:T(8,128)(2,1)S(1)} %get-tuple-element.73, bf16[512,1152]{1,0:T(8,128)(2,1)} %collective-permute-done.5, bf16[512,1152]{1,0:T(8,128)(2,1)} %fusion.65), kind=kOutput, calls=%fused_computation.10 | convolution fusion | flops 5452627968 | bytes 12386304 | tf_op jit(solution)/shard_map/td,tf->df/dot_general | solution.py:117
  231.1 4.5 pad_maximum_fusion
  235.6 8.2 %convert_add_fusion.2 = f32[512,1152]{1,0:T(8,128)} fusion(bf16[512,1152]{1,0:T(8,128)(2,1)} %collective-permute-done.6, bf16[512,2304]{1,0:T(8,128)(2,1)} %copy-done.58, bf16[1152,4608]{1,0:T(8,128)(2,1)} %all-gather.6.cloned.1.call-done), kind=kOutput, calls=%fused_computation.116 | convolution fusion | flops 2719088640 | bytes 11206656 | tf_op jit(solution)/shard_map/tf,df->td/dot_general | solution.py:117
  244.6 6.6 %fusion.40 = bf16[512,1152]{1,0:T(8,128)(2,1)S(1)} fusion(bf16[512,2304]{1,0:T(8,128)(2,1)} %get-tuple-element.75, bf16[1152,4608]{1,0:T(8,128)(2,1)} %all-gather.6.cloned.1.call-done), kind=kOutput, calls=%fused_computation.67 | convolution fusion | flops 2718498816 | bytes 8847360 | tf_op jit(solution)/shard_map/tf,df->td/dot_general | solution.py:117
  251.9 6.8 %fusion.27 = f32[512,1152]{1,0:T(8,128)S(1)} fusion(bf16[512,2304]{1,0:T(8,128)(2,1)S(1)} %copy-done.60, bf16[1152,4608]{1,0:T(8,128)(2,1)} %all-gather.6.cloned.1.call-done), kind=kOutput, calls=%fused_computation.55 | convolution fusion | flops 2717908992 | bytes 10027008 | tf_op jit(solution)/shard_map/tf,df->td/dot_general | solution.py:117
  260.3 15.6 %collective-permute-done.4 = bf16[512,1152]{1,0:T(8,128)(2,1)S(1)} collective-permute-done((bf16[512,1152]{1,0:T(8,128)(2,1)S(1)}, bf16[512,1152]{1,0:T(8,128)(2,1)S(1)}, u32[]{:S(2)}, u32[]{:S(2)}) %collective-permute-start.4) | collective-permute-done | bytes 1179680 | tf_op jit(solution)/shard_map/ppermute | solution.py:91
  275.9 4.1 fusion.66
  282.2 13.3 %fusion.134 = f32[8,1024,1024]{2,1,0:T(8,128)} fusion(bf16[1024,8,72]{0,2,1:T(8,128)(2,1)S(1)} %bitcast.145, bf16[1024,8,72]{0,2,1:T(8,128)(2,1)S(1)} %bitcast.140), kind=kOutput, calls=%fused_computation.218 | convolution fusion | flops 1207959552 | bytes 35913728 | tf_op jit(solution)/shard_map/qhd,khd->hqk/dot_general | solution.py:74
  297.1 8.3 %collective-permute-done.7 = bf16[512,1152]{1,0:T(8,128)(2,1)S(1)} collective-permute-done((bf16[512,1152]{1,0:T(8,128)(2,1)S(1)}, bf16[512,1152]{1,0:T(8,128)(2,1)S(1)}, u32[]{:S(2)}, u32[]{:S(2)}) %collective-permute-start.7) | collective-permute-done | bytes 1179680 | tf_op jit(solution)/shard_map/ppermute | solution.py:91
  307.5 2.8 convolution_convert_fusion.3
  310.3 19.7 %multiply_convert_fusion = bf16[8,1024,1024]{2,1,0:T(8,128)(2,1)} fusion(f32[8,1024,1024]{2,1,0:T(8,128)} %fusion.134, f32[8,1024]{1,0:T(8,128)S(1)} %bitcast.170, f32[8,1024]{1,0:T(8,128)S(1)} %pad_maximum_fusion.7, bf16[1024,8,72]{0,2,1:T(8,128)(2,1)S(1)} %bitcast.143, bf16[1024,8,72]{0,2,1:T(8,128)(2,1)S(1)} %bitcast.149), kind=kOutput, calls=%fused_computation | convolution fusion | flops 1258291200 | bytes 52756480 | tf_op jit(solution)/shard_map/qhd,khd->hqk/dot_general | solution.py:80
  330.0 9.1 %convolution_convert_fusion.8 = bf16[8,72,1024]{2,1,0:T(8,128)(2,1)S(1)} fusion(bf16[1024,8,72]{0,2,1:T(8,128)(2,1)S(1)} %bitcast.146, bf16[8,1024,1024]{2,1,0:T(8,128)(2,1)} %multiply_convert_fusion), kind=kOutput, calls=%fused_computation.128 | convolution fusion | flops 1208549376 | bytes 19136512 | tf_op jit(solution)/shard_map/hqk,qhd->khd/dot_general | solution.py:86
  339.1 12.1 %convolution_convert_fusion.9 = bf16[8,72,1024]{2,1,0:T(8,128)(2,1)} fusion(bf16[1024,8,72]{0,2,1:T(8,128)(2,1)S(1)} %bitcast.141, bf16[8,1024,1024]{2,1,0:T(8,128)(2,1)} %multiply_convert_fusion), kind=kOutput, calls=%fused_computation.129 | convolution fusion | flops 1208549376 | bytes 19136512 | tf_op jit(solution)/shard_map/hqk,khd->qhd/dot_general | solution.py:85
  351.2 13.2 %fusion.85 = bf16[8,72,1024]{2,1,0:T(8,128)(2,1)S(1)} fusion(bf16[1024,8,72]{0,2,1:T(8,128)(2,1)S(1)} %bitcast.144, f32[8,1024,1024]{2,1,0:T(8,128)} %fusion.134, f32[8,1024]{1,0:T(8,128)} %copy-done.29), kind=kOutput, calls=%fused_computation.127 | convolution fusion | flops 1233715200 | bytes 35946496 | tf_op jit(solution)/shard_map/hqk,qhd->khd/dot_general | solution.py:77
  364.4 9.1 %convolution_convert_fusion.2 = bf16[1152,1728]{0,1:T(8,128)(2,1)S(1)} fusion(bf16[512,1152]{1,0:T(8,128)(2,1)} %copy-done.57, bf16[512,1152]{1,0:T(8,128)(2,1)} %copy-done.26, bf16[1024,576]{0,1:T(8,128)(2,1)S(1)} %bitcast.150, bf16[1024,576]{0,1:T(8,128)(2,1)S(1)} %bitcast.155, bf16[1024,576]{0,1:T(8,128)(2,1)S(1)} %bitcast.157), kind=kOutput, calls=%fused_computation.15 | convolution fusion | flops 4094189568 | bytes 9879552 | tf_op jit(solution)/shard_map/td,tc->dc/dot_general | solution.py:117
  373.6 2.8 pad_maximum_fusion.1
  378.6 8.6 %copy.25 = bf16[1152,2304]{1,0:T(8,128)(2,1)} copy(bf16[1152,2304]{0,1:T(8,128)(2,1)} %pad_maximum_fusion.1) | data formatting | bytes 10616832
  389.2 5.2 convolution_convert_fusion.4
  398.0 19.8 %collective-permute-done.8 = bf16[512,1152]{1,0:T(8,128)(2,1)S(1)} collective-permute-done((bf16[512,1152]{1,0:T(8,128)(2,1)S(1)}, bf16[512,1152]{1,0:T(8,128)(2,1)S(1)}, u32[]{:S(2)}, u32[]{:S(2)}) %collective-permute-start.8) | collective-permute-done | bytes 1179680 | tf_op jit(solution)/shard_map/ppermute | solution.py:91
  417.8 5.3 %fusion.63 = (f32[1152]{0:T(1024)S(1)}, f32[512]{0:T(512)}, f32[512]{0:T(512)}, f32[1152]{0:T(1024)S(1)}, f32[512,1152]{1,0:T(8,128)}) fusion(bf16[1,512,1152]{2,1,0:T(8,128)(2,1)S(1)} %copy-done.4, f32[512]{0:T(512)S(1)} %copy-done.53, f32[512]{0:T(512)S(1)} %copy-done.50, f32[1152]{0:T(1024)S(1)} %copy-done.38, ...), kind=kOutput, calls=%fused_computation.94 | convolution fusion | flops 2045506304 | bytes 10642432 | tf_op jit(solution)/shard_map/tc,dc->td/dot_general | solution.py:117
  432.7 8.6 %all-to-all-start.1 = ((f32[16,1,432]{2,1,0:T(1,128)}), f32[16,1,432]{2,1,0:T(1,128)}, u32[]{:S(2)}, u32[]{:S(2)}) async-start(f32[16,1,432]{2,1,0:T(1,128)} %all_to_all.16), calls=%async_computation.1 | async-start | bytes 65536 | tf_op jit(solution)/shard_map/all_to_all | solution.py:243
  441.3 3.9 fusion.62
  445.2 2.8 all-to-all-done.1
  449.4 59.8 %psum.7 = f32[16,576]{1,0:T(8,128)S(1)} all-reduce(f32[16,576]{1,0:T(8,128)S(1)} %fusion.110), channel_id=1, replica_groups=mesh['dp'=16,'tensor'=2] {'dp'}, use_global_device_ids=true, to_apply=%region_19.20 | all-reduce | flops 9216 | bytes 73728 | tf_op jit(solution)/shard_map/psum | solution.py:247
  511.7 3.3 fusion.101
  (223 shorter events, 58.8 us)
Async XLA Ops:
  7.2 29.9 %copy-start = (bf16[1000,576]{0,1:T(8,128)(2,1)S(1)}, bf16[1000,576]{0,1:T(8,128)(2,1)}, u32[]{:S(2)}) copy-start(bf16[1000,576]{0,1:T(8,128)(2,1)} %param.13) | copy-start | bytes 3456004
  7.2 30.4 %copy-start.24 = (bf16[576,432]{0,1:T(8,128)(2,1)S(1)}, bf16[576,432]{0,1:T(8,128)(2,1)}, u32[]{:S(2)}) copy-start(bf16[576,432]{0,1:T(8,128)(2,1)} %param.14) | copy-start | bytes 1492996
  7.2 75.1 %all-gather.4.cloned.1.call-start = ((), (), s32[]{:S(2)}) async-start(), calls=%async_computation.4 | async-start | bytes 5640192 | tf_op jit(solution)/shard_map/all_gather | solution.py:138
  8.4 31.3 %copy-start.2 = (bf16[1,512,1152]{2,1,0:T(8,128)(2,1)S(1)}, bf16[1,512,1152]{2,1,0:T(8,128)(2,1)}, u32[]{:S(2)}) copy-start(bf16[1,512,1152]{2,1,0:T(8,128)(2,1)} %param.10) | copy-start | bytes 3538948
  10.3 157.8 %all-gather.6.cloned.1.call-start = ((), (), s32[]{:S(2)}) async-start(), calls=%async_computation.5 | async-start | bytes 11280384 | tf_op jit(solution)/shard_map/all_gather | solution.py:144
  38.2 3.9 collective-permute-start
  39.9 47.6 %copy-start.49 = (f32[512]{0:T(512)}, f32[512]{0:T(512)S(1)}, u32[]{:S(2)}) copy-start(f32[512]{0:T(512)S(1)} %broadcast_multiply_fusion.5) | copy-start | bytes 6148
  42.8 10.7 %all-to-all-start = ((f32[16,1,432]{2,1,0:T(1,128)}), f32[16,1,432]{2,1,0:T(1,128)S(1)}, u32[]{:S(2)}, u32[]{:S(2)}) async-start(f32[16,1,432]{2,1,0:T(1,128)} %copy.22), calls=%async_computation | async-start | bytes 65536 | tf_op jit(solution)/shard_map/all_to_all | solution.py:155
  46.3 330.1 %reduce-scatter.5.cloned.1.call-start = ((), (), s32[]{:S(2)}) async-start(), calls=%async_computation.6 | async-start | bytes 11280384 | tf_op jit(solution)/shard_map/reduce_scatter | solution.py:199
  46.3 41.2 %copy-start.52 = (f32[512]{0:T(512)}, f32[512]{0:T(512)S(1)}, u32[]{:S(2)}) copy-start(f32[512]{0:T(512)S(1)} %add_rsqrt_fusion.1) | copy-start | bytes 6148
  54.9 32.6 %copy-start.26 = (bf16[512,1152]{1,0:T(8,128)(2,1)}, bf16[512,1152]{1,0:T(8,128)(2,1)S(1)}, u32[]{:S(2)}) copy-start(bf16[512,1152]{1,0:T(8,128)(2,1)S(1)} %fusion.57) | copy-start | bytes 3538948
  55.0 27.4 %collective-permute-start.1 = (bf16[512,1152]{1,0:T(8,128)(2,1)S(1)}, bf16[512,1152]{1,0:T(8,128)(2,1)S(1)}, u32[]{:S(2)}, u32[]{:S(2)}) collective-permute-start(bf16[512,1152]{1,0:T(8,128)(2,1)S(1)} %fusion.57), channel_id=1, source_target_pairs={{0,1},{1,0},{2,3},{3,2},{4,5},{5,4},{6,7},{7,6},{8,9},{9,8},{10,11... | collective-permute-start | bytes 3538952 | tf_op jit(solution)/shard_map/ppermute | solution.py:91
  93.4 20.6 %copy-start.8 = (bf16[1024,576]{0,1:T(8,128)(2,1)}, bf16[1024,576]{0,1:T(8,128)(2,1)S(1)}, u32[]{:S(2)}) copy-start(bf16[1024,576]{0,1:T(8,128)(2,1)S(1)} %get-tuple-element.55) | copy-start | bytes 3538948
  106.4 26.6 %collective-permute-start.2 = (bf16[512,1152]{1,0:T(8,128)(2,1)S(1)}, bf16[512,1152]{1,0:T(8,128)(2,1)S(1)}, u32[]{:S(2)}, u32[]{:S(2)}) collective-permute-start(bf16[512,1152]{1,0:T(8,128)(2,1)S(1)} %convolution_convert_fusion.5), channel_id=1, source_target_pairs={{0,1},{1,0},{2,3},{3,2},{4,5},{5,4},{6,7},{7,6},{8,9},{9,8},{10,11... | collective-permute-start | bytes 3538952 | tf_op jit(solution)/shard_map/ppermute | solution.py:91
  114.1 18.9 %copy-start.3 = (bf16[1,512,1152]{2,1,0:T(8,128)(2,1)S(1)}, bf16[1,512,1152]{2,1,0:T(8,128)(2,1)}, u32[]{:S(2)}) copy-start(bf16[1,512,1152]{2,1,0:T(8,128)(2,1)} %param.10) | copy-start | bytes 3538948
  114.1 18.9 %copy-start.39 = (f32[1152]{0:T(1024)S(1)}, f32[1152]{0:T(1024)}, u32[]{:S(2)}) copy-start(f32[1152]{0:T(1024)} %get-tuple-element.45) | copy-start | bytes 13828
  118.2 19.7 %copy-start.13 = (bf16[8,72,512]{2,1,0:T(8,128)(2,1)}, bf16[8,72,512]{2,1,0:T(8,128)(2,1)S(1)}, u32[]{:S(2)}) copy-start(bf16[8,72,512]{2,1,0:T(8,128)(2,1)S(1)} %fusion.89) | copy-start | bytes 1769476
  139.1 29.0 %collective-permute-start.3 = (bf16[512,1152]{1,0:T(8,128)(2,1)S(1)}, bf16[512,1152]{1,0:T(8,128)(2,1)}, u32[]{:S(2)}, u32[]{:S(2)}) collective-permute-start(bf16[512,1152]{1,0:T(8,128)(2,1)S(1)} %add_convert_fusion.1), channel_id=1, source_target_pairs={{0,1},{1,0},{2,3},{3,2},{4,5},{5,4},{6,7},{7,6},{8,9},{9,8},{10,11... | collective-permute-start | bytes 3538952 | tf_op jit(solution)/shard_map/ppermute | solution.py:91
  141.9 48.4 %collective-permute-start.5 = (bf16[512,1152]{1,0:T(8,128)(2,1)}, bf16[512,1152]{1,0:T(8,128)(2,1)}, u32[]{:S(2)}, u32[]{:S(2)}) collective-permute-start(bf16[512,1152]{1,0:T(8,128)(2,1)} %fusion.65), channel_id=1, source_target_pairs={{0,1},{1,0},{2,3},{3,2},{4,5},{5,4},{6,7},{7,6},{8,9},{9,8},{10,11... | collective-permute-start | bytes 3538952 | tf_op jit(solution)/shard_map/ppermute | solution.py:91
  168.1 22.2 %copy-start.56 = (bf16[1152,4608]{1,0:T(8,128)(2,1)S(1)}, bf16[1152,4608]{1,0:T(8,128)(2,1)}, u32[]{:S(2)}) copy-start(bf16[1152,4608]{1,0:T(8,128)(2,1)} %all-gather.6.cloned.1.call-done) | copy-start | bytes 31850500
  201.2 34.4 %collective-permute-start.6 = (bf16[512,1152]{1,0:T(8,128)(2,1)}, bf16[512,1152]{1,0:T(8,128)(2,1)}, u32[]{:S(2)}, u32[]{:S(2)}) collective-permute-start(bf16[512,1152]{1,0:T(8,128)(2,1)} %fusion.37), channel_id=1, source_target_pairs={{0,1},{1,0},{2,3},{3,2},{4,5},{5,4},{6,7},{7,6},{8,9},{9,8},{10,11... | collective-permute-start | bytes 3538952 | tf_op jit(solution)/shard_map/ppermute | solution.py:91
  206.5 16.6 %copy-start.59 = (bf16[512,2304]{1,0:T(8,128)(2,1)}, bf16[512,2304]{1,0:T(8,128)(2,1)S(1)}, u32[]{:S(2)}) copy-start(bf16[512,2304]{1,0:T(8,128)(2,1)S(1)} %get-tuple-element.73) | copy-start | bytes 7077892
  243.8 272.4 %reduce-scatter.7.cloned.1.call-start = ((), (), s32[]{:S(2)}) async-start(), calls=%async_computation.7 | async-start | bytes 5640192
  244.6 65.7 %copy-start.29 = (f32[8,1024]{1,0:T(8,128)}, f32[8,1024]{1,0:T(8,128)S(1)}, u32[]{:S(2)}) copy-start(f32[8,1024]{1,0:T(8,128)S(1)} %pad_maximum_fusion.7) | copy-start | bytes 98308
  251.2 24.7 %collective-permute-start.4 = (bf16[512,1152]{1,0:T(8,128)(2,1)S(1)}, bf16[512,1152]{1,0:T(8,128)(2,1)S(1)}, u32[]{:S(2)}, u32[]{:S(2)}) collective-permute-start(bf16[512,1152]{1,0:T(8,128)(2,1)S(1)} %fusion.40), channel_id=1, source_target_pairs={{0,1},{1,0},{2,3},{3,2},{4,5},{5,4},{6,7},{7,6},{8,9},{9,8},{10,11... | collective-permute-start | bytes 3538952 | tf_op jit(solution)/shard_map/ppermute | solution.py:91
  258.7 17.2 %copy-start.11 = (f32[512,1152]{1,0:T(8,128)S(1)}, f32[512,1152]{1,0:T(8,128)}, u32[]{:S(2)}) copy-start(f32[512,1152]{1,0:T(8,128)} %get-tuple-element.72) | copy-start | bytes 7077892
  258.7 17.2 %copy-start.16 = (bf16[512,1152]{1,0:T(8,128)(2,1)S(1)}, bf16[512,1152]{1,0:T(8,128)(2,1)}, u32[]{:S(2)}) copy-start(bf16[512,1152]{1,0:T(8,128)(2,1)} %copy-done.15) | copy-start | bytes 3538948
  258.7 17.2 %copy-start.20 = (bf16[1,512,1152]{2,1,0:T(8,128)(2,1)S(1)}, bf16[1,512,1152]{2,1,0:T(8,128)(2,1)}, u32[]{:S(2)}) copy-start(bf16[1,512,1152]{2,1,0:T(8,128)(2,1)} %param.19) | copy-start | bytes 3538948
  258.7 17.2 %copy-start.36 = (f32[1152]{0:T(1024)S(1)}, f32[1152]{0:T(1024)}, u32[]{:S(2)}) copy-start(f32[1152]{0:T(1024)} %get-tuple-element.40) | copy-start | bytes 13828
  275.9 19.6 %slice-start.1 = ((s8[5308416]{0:T(1024)(128)(4,1)}), s8[4194304]{0:T(1024)(128)(4,1)S(1)}, s32[]{:S(2)}) async-start(s8[5308416]{0:T(1024)(128)(4,1)} %bitcast.164), calls=%async_computation.9 | async-start | bytes 8388608
  281.6 23.8 %collective-permute-start.7 = (bf16[512,1152]{1,0:T(8,128)(2,1)S(1)}, bf16[512,1152]{1,0:T(8,128)(2,1)S(1)}, u32[]{:S(2)}, u32[]{:S(2)}) collective-permute-start(bf16[512,1152]{1,0:T(8,128)(2,1)S(1)} %multiply_convert_fusion.3), channel_id=1, source_target_pairs={{0,1},{1,0},{2,3},{3,2},{4,5},{5,4},{6,7},{7,6},{8,9},{9,8},{10,11... | collective-permute-start | bytes 3538952 | tf_op jit(solution)/shard_map/ppermute | solution.py:91
  282.2 13.3 %slice-start.2 = ((s8[5308416]{0:T(1024)(128)(4,1)}), s8[1114112]{0:T(1024)(128)(4,1)S(1)}, s32[]{:S(2)}) async-start(s8[5308416]{0:T(1024)(128)(4,1)} %bitcast.164), calls=%async_computation.10 | async-start | bytes 2228224
  297.1 10.0 %copy-start.14 = (bf16[8,72,512]{2,1,0:T(8,128)(2,1)S(1)}, bf16[8,72,512]{2,1,0:T(8,128)(2,1)}, u32[]{:S(2)}) copy-start(bf16[8,72,512]{2,1,0:T(8,128)(2,1)} %copy-done.13) | copy-start | bytes 1769476
  297.1 10.0 %copy-start.23 = (bf16[8,72,512]{2,1,0:T(8,128)(2,1)S(1)}, bf16[8,72,512]{2,1,0:T(8,128)(2,1)}, u32[]{:S(2)}) copy-start(bf16[8,72,512]{2,1,0:T(8,128)(2,1)} %copy-done.22) | copy-start | bytes 1769476
  351.2 13.2 %copy-start.17 = (bf16[8,72,1024]{2,1,0:T(8,128)(2,1)S(1)}, bf16[8,72,1024]{2,1,0:T(8,128)(2,1)}, u32[]{:S(2)}) copy-start(bf16[8,72,1024]{2,1,0:T(8,128)(2,1)} %convolution_convert_fusion.9) | copy-start | bytes 3538948
  388.4 29.3 %slice-start.3 = ((s8[5308416]{0:T(1024)(128)(4,1)}), s8[4194304]{0:T(1024)(128)(4,1)S(1)}, s32[]{:S(2)}) async-start(s8[5308416]{0:T(1024)(128)(4,1)} %bitcast.166), calls=%async_computation.11 | async-start | bytes 8388608
  389.1 28.6 %copy-start.4 = (bf16[1,512,1152]{2,1,0:T(8,128)(2,1)S(1)}, bf16[1,512,1152]{2,1,0:T(8,128)(2,1)}, u32[]{:S(2)}) copy-start(bf16[1,512,1152]{2,1,0:T(8,128)(2,1)} %param.10) | copy-start | bytes 3538948
  389.1 28.6 %slice-start.4 = ((s8[5308416]{0:T(1024)(128)(4,1)}), s8[1114112]{0:T(1024)(128)(4,1)S(1)}, s32[]{:S(2)}) async-start(s8[5308416]{0:T(1024)(128)(4,1)} %bitcast.166), calls=%async_computation.12 | async-start | bytes 2228224
  389.1 28.6 %copy-start.38 = (f32[1152]{0:T(1024)S(1)}, f32[1152]{0:T(1024)}, u32[]{:S(2)}) copy-start(f32[1152]{0:T(1024)} %copy-done.37) | copy-start | bytes 13828
  389.1 28.6 %copy-start.50 = (f32[512]{0:T(512)S(1)}, f32[512]{0:T(512)}, u32[]{:S(2)}) copy-start(f32[512]{0:T(512)} %copy-done.49) | copy-start | bytes 6148
  389.2 28.6 %copy-start.53 = (f32[512]{0:T(512)S(1)}, f32[512]{0:T(512)}, u32[]{:S(2)}) copy-start(f32[512]{0:T(512)} %copy-done.52) | copy-start | bytes 6148
  394.3 23.4 %collective-permute-start.8 = (bf16[512,1152]{1,0:T(8,128)(2,1)S(1)}, bf16[512,1152]{1,0:T(8,128)(2,1)S(1)}, u32[]{:S(2)}, u32[]{:S(2)}) collective-permute-start(bf16[512,1152]{1,0:T(8,128)(2,1)S(1)} %convolution_convert_fusion.4), channel_id=1, source_target_pairs={{0,1},{1,0},{2,3},{3,2},{4,5},{5,4},{6,7},{7,6},{8,9},{9,8},{10,11... | collective-permute-start | bytes 3538952 | tf_op jit(solution)/shard_map/ppermute | solution.py:91
  397.9 43.4 %copy-start.6 = (f32[512,1152]{1,0:T(8,128)S(1)}, f32[512,1152]{1,0:T(8,128)}, u32[]{:S(2)}) copy-start(f32[512,1152]{1,0:T(8,128)} %copy-done.5) | copy-start | bytes 7077892
  398.0 43.4 %copy-start.51 = (f32[512]{0:T(512)S(1)}, f32[512]{0:T(512)}, u32[]{:S(2)}) copy-start(f32[512]{0:T(512)} %copy-done.49) | copy-start | bytes 6148
  398.0 43.4 %copy-start.54 = (f32[512]{0:T(512)S(1)}, f32[512]{0:T(512)}, u32[]{:S(2)}) copy-start(f32[512]{0:T(512)} %copy-done.52) | copy-start | bytes 6148
  427.2 4.1 collective-permute-start.9
  432.7 15.3 %all-to-all-start.1 = ((f32[16,1,432]{2,1,0:T(1,128)}), f32[16,1,432]{2,1,0:T(1,128)}, u32[]{:S(2)}, u32[]{:S(2)}) async-start(f32[16,1,432]{2,1,0:T(1,128)} %all_to_all.16), calls=%async_computation.1 | async-start | bytes 65536 | tf_op jit(solution)/shard_map/all_to_all | solution.py:243
  445.2 69.8 %copy-start.12 = (f32[72,4608]{1,0:T(8,128)S(1)}, f32[72,4608]{1,0:T(8,128)}, u32[]{:S(2)}) copy-start(f32[72,4608]{1,0:T(8,128)} %convert_element_type.207) | copy-start | bytes 3981316
  (36 other events, 162.0 us)
Sparse Core Ops, SparseCore 0:
  10.7 59.4 all-gather.3
  73.0 86.9 all-gather.5
  243.9 120.1 reduce-scatter.4
  387.3 80.5 reduce-scatter.6

commit v2 on v1

--- a/solution.py
+++ b/solution.py
@@ -1,10 +1,10 @@
-import functools
 import math
 
 import jax
 import jax.numpy as jnp
 from jax import lax
 from jax.sharding import PartitionSpec as P
+
 
 D = 1152
 H = 16
@@ -113,6 +113,18 @@
     return total
 
 
+def spread(value, groups):
+    return lax.all_to_all(jnp.tile(value, (groups, 1)), "dp", 0, 0, tiled=True)
+
+
+def sum_groups(value, groups):
+    rows, width = value.shape
+    cut = value.reshape(rows, groups, width // groups).swapaxes(0, 1)
+    got = lax.all_to_all(cut, "dp", 0, 0, tiled=True)
+    whole = spread(jnp.sum(got, axis=0), groups)
+    return whole.reshape(groups, rows, width // groups).swapaxes(0, 1).reshape(rows, width)
+
+
 def dot(spec, left, right):
     return jnp.einsum(spec, left, right, preferred_element_type=jnp.float32)
 
@@ -122,7 +134,7 @@
 
 
 def shards(
-    ranks, latents_in, steps, labels, class_table, w_ada, w_qkv, w_proj, w_fc1, w_fc2, cotangent
+    ranks, groups, latents_in, steps, labels, class_table, w_ada, w_qkv, w_proj, w_fc1, w_fc2, cotangent
 ):
     half = jnp.bfloat16
     rank = lax.axis_index("tensor")
@@ -133,7 +145,7 @@
     heads_here = owned // head_size
     score_scale = head_size ** (-0.5)
     highest = lax.Precision.HIGHEST
-    marks = lax.all_gather(jnp.stack([steps, labels], axis=1), "dp", axis=0, tiled=True)
+    marks = spread(jnp.stack([steps, labels], axis=1), groups)
     all_steps, all_labels = marks[:, 0], marks[:, 1]
     attn_w = lax.all_gather(
         jnp.concatenate([w_qkv[0], w_qkv[1], w_qkv[2], w_proj.T], axis=1),
@@ -162,6 +174,7 @@
     rest_a = fetch_rest(mod_a, ranks)
     grad_out = cotangent[0].astype(jnp.float32)
     grad_mlp = (grad_out * gate_m).astype(half)
+    grad_mlp, rest_a = lax.optimization_barrier((grad_mlp, rest_a))
     rest_grad_m = fetch_rest(grad_mlp, ranks)
     qkv_own = dot("td,dc->tc", mod_a, qkv_full).astype(half)
     qkv_rest = dot("td,dc->tc", rest_a, qkv_full).astype(half)
@@ -172,7 +185,9 @@
     values = projected[:, 2 * owned :].reshape(tokens, heads_here, head_size)
     mixed_rest, log_rest = attend(queries[mine:], keys, values, score_scale)
     mixed_rest_flat = mixed_rest.reshape(tokens - mine, owned)
-    attn_away = return_rest(dot("tc,dc->td", mixed_rest_flat, proj_t), ranks)
+    attn_rest = dot("tc,dc->td", mixed_rest_flat, proj_t).astype(half)
+    attn_rest, rest_grad_m = lax.optimization_barrier((attn_rest, rest_grad_m))
+    attn_away = return_rest(attn_rest, ranks)
     mixed_own, log_own = attend(queries[:mine], keys, values, score_scale)
     mixed_own_flat = mixed_own.reshape(mine, owned)
     attn_out = dot("tc,dc->td", mixed_own_flat, proj_t) + attn_away
@@ -182,15 +197,17 @@
     rest_m = fetch_rest(mod_m, ranks)
     pre_own = dot("td,df->tf", mod_m, fc1_full)
     acts_own = gelu_value(pre_own).astype(half)
+    grad_pre_own = (dot("td,df->tf", grad_mlp, fc2_t) * gelu_slope(pre_own)).astype(half)
+    acts_own, grad_pre_own, rest_m = lax.optimization_barrier((acts_own, grad_pre_own, rest_m))
     pre_rest = dot("td,df->tf", rest_m, fc1_full)
     acts_rest = gelu_value(pre_rest).astype(half)
-    mlp_away = return_rest(dot("tf,df->td", acts_rest, fc2_t), ranks)
     grad_pre_rest = (dot("td,df->tf", rest_grad_m, fc2_t) * gelu_slope(pre_rest)).astype(half)
-    grad_mod_away = return_rest(dot("tf,df->td", grad_pre_rest, fc1_full), ranks)
+    grad_mod_rest = dot("tf,df->td", grad_pre_rest, fc1_full).astype(half)
+    grad_mod_rest, acts_rest = lax.optimization_barrier((grad_mod_rest, acts_rest))
+    grad_mod_away = return_rest(grad_mod_rest, ranks)
+    mlp_rest = dot("tf,df->td", acts_rest, fc2_t).astype(half)
+    mlp_away = return_rest(mlp_rest, ranks)
     mlp_out = dot("tf,df->td", acts_own, fc2_t) + mlp_away
-    block_out = (hidden + gate_m * mlp_out).astype(half)
-    grad_gate_m = jnp.sum(grad_out * mlp_out, axis=0)
-    grad_pre_own = (dot("td,df->tf", grad_mlp, fc2_t) * gelu_slope(pre_own)).astype(half)
     grad_mod_m = dot("tf,df->td", grad_pre_own, fc1_full) + grad_mod_away
     grad_fc2_t = dot("td,tf->df", join(grad_mlp, rest_grad_m), join(acts_own, acts_rest))
     grad_fc1 = dot("td,tf->df", join(mod_m, rest_m), join(grad_pre_own, grad_pre_rest))
@@ -202,6 +219,8 @@
         scatter_dimension=0,
         tiled=True,
     ).astype(jnp.float32)
+    block_out = (hidden + gate_m * mlp_out).astype(half)
+    grad_gate_m = jnp.sum(grad_out * mlp_out, axis=0)
     grad_shift_m = jnp.sum(grad_mod_m, axis=0)
     grad_scale_m = jnp.sum(grad_mod_m * normed_m, axis=0)
     grad_hidden = grad_out + norm_back(grad_mod_m * (1.0 + scale_m), normed_m, inv_m)
@@ -244,9 +263,9 @@
     grad_ada = jnp.einsum(
         "lc,lm->cm", cond_half.astype(jnp.float32), grad_modulation, precision=highest
     )
-    grad_cond = lax.psum(
+    grad_cond = sum_groups(
         jnp.einsum("lm,cm->lc", grad_modulation, w_ada.astype(jnp.float32), precision=highest),
-        "dp",
+        groups,
     ) * silu_slope(cond)
     grad_table = jnp.einsum("ln,lc->nc", one_hot.astype(jnp.float32), grad_cond, precision=highest)
     return (
@@ -262,8 +281,11 @@
 
 
 def solution(mesh):
+    def body(*operands):
+        return shards(mesh.shape["tensor"], mesh.shape["dp"], *operands)
+
     return jax.shard_map(
-        functools.partial(shards, mesh.shape["tensor"]),
+        body,
         mesh=mesh,
         in_specs=(
             P("dp", "tensor", None),

time: 534 us -> 503 us (0.942)
  blocking collectives: 83.1 us -> 0 us
  waiting for transfers between devices: 137 us -> 163 us
  starting transfers between devices: 23.1 us -> 39.1 us
  local copies, waits for them, and re-layouts: 27.7 us -> 33.7 us
  matrix products: 198 us -> 204 us
    psum x1 -> x0, blocking collectives: 59.8 us -> none  [shards(): lax.psum(jnp.einsum('lm,cm->lc', grad_modulation, w_ada.astype(jnp.float3...]
    all_gather x1, waiting for transfers between devices: 0.01 us -> 24.6 us  [shards(): lax.all_gather(jnp.concatenate([w_fc1, w_fc2.T], axis=1), 'dp', axis=0, t...]
    all_gather x1 -> x0, blocking collectives: 23.3 us -> none  [shards(): lax.all_gather(jnp.stack([steps, labels], axis=1), 'dp', axis=0, tiled=True)]
    all_to_all x0 -> x3, starting transfers between devices: none -> 15.3 us  [the longest x2 11.2 us: spread(): return lax.all_to_all(jnp.tile(value, (groups, 1)), 'dp', 0, 0, tiled=True)]
    ppermute x10, waiting for transfers between devices: 127 us -> 113 us  [from_rank(): lax.ppermute(value, 'tensor', [(i, (i - step) % ranks) for i in range(ran...]
    all_to_all x0 -> x3, waiting for transfers between devices: none -> 13.1 us  [the longest x2 10.3 us: spread(): return lax.all_to_all(jnp.tile(value, (groups, 1)), 'dp', 0, 0, tiled=True)]
    unnamed x138 -> x143, local copies, waits for them, and re-layouts: 15.4 us -> 19.3 us
  transfers between devices with their start and end apart: 16 -> 19, of which waited for: 11 -> 15; matrix products, arithmetic and copies ran while one was open for 43% -> 44% of each run, Pallas kernels for 0% -> 0%
where the time goes in v2:
time: 503 us; the launch traced here: 495 us
  matrix products  204 us (41%)
  waiting for transfers between devices  163 us (32%)
  starting transfers between devices  39.1 us (8%)
  other arithmetic  39 us (8%)
  local copies, waits for them, and re-layouts  33.7 us (7%)
  between operations  16.4 us (3%)
    dot_general x20, matrix products, dot(): return jnp.einsum(spec, left, right, preferred_element_type=jnp.float32)  115 us
    ppermute x10, waiting for transfers between devices, from_rank(): lax.ppermute(value, 'tensor', [(i, (i - step) % ranks) for i in range(ran...  113 us
    all_gather x1, waiting for transfers between devices, shards(): lax.all_gather(jnp.concatenate([w_fc1, w_fc2.T], axis=1), 'dp', axis=0, t...  24.6 us
    dot_general x1, matrix products, attend_back(): jnp.einsum('qhd,khd->hqk', grad_mixed, values, preferred_element_type=jnp...  19.8 us
    unnamed x143, local copies, waits for them, and re-layouts  19.3 us
    ppermute x10, starting transfers between devices, from_rank(): lax.ppermute(value, 'tensor', [(i, (i - step) % ranks) for i in range(ran...  15.3 us
    dot_general x1, matrix products, attend_back(): jnp.einsum('qhd,khd->hqk', queries, keys, preferred_element_type=jnp.floa...  13.8 us
    dot_general x1, matrix products, attend_back(): jnp.einsum('hqk,qhd->khd', probs.astype(jnp.bfloat16), grad_mixed, prefer...  13.4 us
  transfers between devices with their start and end apart: 19, of which 15 were waited for; matrix products, arithmetic and copies ran while one was open for 44% of the time, Pallas kernels for 0%

profile of v2, /device:TPU:0, one launch (start us, length us, event | category | flops | bytes accessed | tf_op | source)
XLA Modules:
  0.0 495.2 jit_solution(2714096623441295708)
XLA Ops:
  14.3 7.4 %all-to-all-start = ((s32[16,1,2]{2,1,0:T(1,128)}), s32[16,1,2]{2,1,0:T(1,128)S(1)}, u32[]{:S(2)}, u32[]{:S(2)}) async-start(s32[16,1,2]{2,1,0:T(1,128)} %tile.4), calls=%async_computation | async-start | bytes 16384 | tf_op jit(solution)/shard_map/all_to_all | solution.py:117
  22.0 6.1 %all-to-all-done = s32[16,1,2]{2,1,0:T(1,128)S(1)} async-done(((s32[16,1,2]{2,1,0:T(1,128)}), s32[16,1,2]{2,1,0:T(1,128)S(1)}, u32[]{:S(2)}, u32[]{:S(2)}) %all-to-all-start) | async-done | bytes 160 | tf_op jit(solution)/shard_map/all_to_all | solution.py:117
  33.8 3.5 all-to-all-start.1
  37.4 6.6 %all-to-all-done.1 = f32[16,1,432]{2,1,0:T(1,128)S(1)} async-done(((f32[16,1,432]{2,1,0:T(1,128)}), f32[16,1,432]{2,1,0:T(1,128)S(1)}, u32[]{:S(2)}, u32[]{:S(2)}) %all-to-all-start.1) | async-done | bytes 27680 | tf_op jit(solution)/shard_map/all_to_all | solution.py:167
  47.2 25.7 %collective-permute-done.1 = bf16[512,1152]{1,0:T(8,128)(2,1)S(1)} collective-permute-done((bf16[512,1152]{1,0:T(8,128)(2,1)S(1)}, bf16[512,1152]{1,0:T(8,128)(2,1)S(1)}, u32[]{:S(2)}, u32[]{:S(2)}) %collective-permute-start.1) | collective-permute-done | bytes 1179680 | tf_op jit(solution)/shard_map/ppermute | solution.py:91
  75.4 5.2 %convolution_convert_fusion.6 = bf16[512,1728]{0,1:T(8,128)(2,1)S(1)} fusion(bf16[512,1152]{1,0:T(8,128)(2,1)} %copy-done.61, bf16[1152,2304]{1,0:T(8,128)(2,1)} %all-gather.3.cloned.1.call-done), kind=kOutput, calls=%fused_computation.72 | convolution fusion | flops 2039316480 | bytes 7077888 | tf_op jit(solution)/shard_map/td,dc->tc/dot_general | solution.py:129
  83.3 3.7 pad_maximum_fusion.3
  89.4 3.5 exponential_reduce_fusion
  93.0 3.7 fusion.94
  96.7 3.2 convolution_convert_fusion.5
  104.7 3.5 exponential_reduce_fusion.1
  108.3 3.9 fusion.95
  112.2 14.2 %collective-permute-done.3 = bf16[512,1152]{1,0:T(8,128)(2,1)S(1)} collective-permute-done((bf16[512,1152]{1,0:T(8,128)(2,1)S(1)}, bf16[512,1152]{1,0:T(8,128)(2,1)S(1)}, u32[]{:S(2)}, u32[]{:S(2)}) %collective-permute-start.3) | collective-permute-done | bytes 1179680 | tf_op jit(solution)/shard_map/ppermute | solution.py:91
  126.4 4.9 fusion.137
  135.1 24.6 %all-gather.5.cloned.1.call-done = bf16[1152,4608]{1,0:T(8,128)(2,1)} async-done(((bf16[72,4608]{1,0:T(8,128)(2,1)}), bf16[1152,4608]{1,0:T(8,128)(2,1)}) %all-gather.5.cloned.1.call-update) | async-done | bytes 10616848 | tf_op jit(solution)/shard_map/all_gather | solution.py:156
  159.7 6.9 %multiply_convert_fusion.2 = (bf16[512,2304]{1,0:T(8,128)(2,1)S(1)}, f32[512,2304]{1,0:T(8,128)S(1)}) fusion(bf16[512,1152]{1,0:T(8,128)(2,1)} %add_convert_fusion.1, bf16[1152,4608]{1,0:T(8,128)(2,1)} %all-gather.5.cloned.1.call-done), kind=kOutput, calls=%fused_computation.40 | convolution fusion | flops 2728525824 | bytes 13565952 | tf_op jit(solution)/shard_map/td,df->tf/dot_general | solution.py:129
  166.6 5.4 %fusion.21 = bf16[512,2304]{1,0:T(8,128)(2,1)S(1)} fusion(f32[512,2304]{1,0:T(8,128)S(1)} %get-tuple-element.100, bf16[512,1152]{1,0:T(8,128)(2,1)S(1)} %copy-done.31, bf16[1152,4608]{1,0:T(8,128)(2,1)S(1)} %copy-done.60), kind=kOutput, calls=%fused_computation.41 | convolution fusion | flops 2740322304 | bytes 13565952 | tf_op jit(solution)/shard_map/td,df->tf/dot_general | solution.py:129
  172.0 6.0 %multiply_convert_fusion.1 = (bf16[512,2304]{1,0:T(8,128)(2,1)S(1)}, f32[512,2304]{1,0:T(8,128)S(1)}) fusion(bf16[512,1152]{1,0:T(8,128)(2,1)} %collective-permute-done.4, bf16[1152,4608]{1,0:T(8,128)(2,1)S(1)} %copy-done.60), kind=kOutput, calls=%fused_computation.39 | convolution fusion | flops 2728525824 | bytes 13565952 | tf_op jit(solution)/shard_map/td,df->tf/dot_general | solution.py:129
  178.0 7.7 %fusion.22 = bf16[512,2304]{1,0:T(8,128)(2,1)S(1)} fusion(f32[512,2304]{1,0:T(8,128)S(1)} %get-tuple-element.102, bf16[512,1152]{1,0:T(8,128)(2,1)} %collective-permute-done.2, bf16[1152,4608]{1,0:T(8,128)(2,1)S(1)} %copy-done.60), kind=kOutput, calls=%fused_computation.42 | convolution fusion | flops 2740322304 | bytes 13565952 | tf_op jit(solution)/shard_map/td,df->tf/dot_general | solution.py:129
  185.7 4.3 fusion.43
  190.0 7.9 %convolution_convert_fusion.1 = bf16[1152,2304]{1,0:T(8,128)(2,1)S(1)} fusion(bf16[512,2304]{1,0:T(8,128)(2,1)S(1)} %fusion.22, bf16[512,2304]{1,0:T(8,128)(2,1)S(1)} %fusion.21, bf16[512,1152]{1,0:T(8,128)(2,1)} %collective-permute-done.4, bf16[512,1152]{1,0:T(8,128)(2,1)} %add_convert_fusion.1), kind=kOutput, calls=%fused_computation.11 | convolution fusion | flops 5452627968 | bytes 12386304 | tf_op jit(solution)/shard_map/td,tf->df/dot_general | solution.py:129
  199.4 7.5 %convolution_convert_fusion = bf16[1152,2304]{1,0:T(8,128)(2,1)S(1)} fusion(bf16[512,2304]{1,0:T(8,128)(2,1)S(1)} %get-tuple-element.27, bf16[512,2304]{1,0:T(8,128)(2,1)S(1)} %get-tuple-element.24, bf16[512,1152]{1,0:T(8,128)(2,1)} %collective-permute-done.2, bf16[512,1152]{1,0:T(8,128)(2,1)S(1)} %copy-done.31), kind=kOutput, calls=%fused_computation.10 | convolution fusion | flops 5452627968 | bytes 12386304 | tf_op jit(solution)/shard_map/td,tf->df/dot_general | solution.py:129
  206.9 4.5 pad_maximum_fusion
  211.4 14.9 %collective-permute-done.6 = bf16[512,1152]{1,0:T(8,128)(2,1)} collective-permute-done((bf16[512,1152]{1,0:T(8,128)(2,1)}, bf16[512,1152]{1,0:T(8,128)(2,1)}, u32[]{:S(2)}, u32[]{:S(2)}) %collective-permute-start.6) | collective-permute-done | bytes 1179680 | tf_op jit(solution)/shard_map/ppermute | solution.py:91
  226.3 8.2 %fusion.37 = f32[512,1152]{1,0:T(8,128)} fusion(bf16[512,2304]{1,0:T(8,128)(2,1)} %copy-done.62, bf16[1152,4608]{1,0:T(8,128)(2,1)} %all-gather.5.cloned.1.call-done, bf16[512,1152]{1,0:T(8,128)(2,1)} %collective-permute-done.6), kind=kOutput, calls=%fused_computation.65 | convolution fusion | flops 2719088640 | bytes 11206656 | tf_op jit(solution)/shard_map/tf,df->td/dot_general | solution.py:129
  234.6 6.6 %fusion.46 = bf16[512,1152]{1,0:T(8,128)(2,1)S(1)} fusion(bf16[512,2304]{1,0:T(8,128)(2,1)} %copy-done.64, bf16[1152,4608]{1,0:T(8,128)(2,1)} %all-gather.5.cloned.1.call-done), kind=kOutput, calls=%fused_computation.69 | convolution fusion | flops 2718498816 | bytes 8847360 | tf_op jit(solution)/shard_map/tf,df->td/dot_general | solution.py:129
  244.5 24.0 %collective-permute-done.5 = bf16[512,1152]{1,0:T(8,128)(2,1)S(1)} collective-permute-done((bf16[512,1152]{1,0:T(8,128)(2,1)S(1)}, bf16[512,1152]{1,0:T(8,128)(2,1)S(1)}, u32[]{:S(2)}, u32[]{:S(2)}) %collective-permute-start.5) | collective-permute-done | bytes 1179680 | tf_op jit(solution)/shard_map/ppermute | solution.py:91
  268.6 9.2 %fusion.72 = (f32[1152]{0:T(1024)}, bf16[1,512,1152]{2,1,0:T(8,128)(2,1)}, f32[1152]{0:T(1024)}, f32[512,1152]{1,0:T(8,128)S(1)}) fusion(bf16[1,512,1152]{2,1,0:T(8,128)(2,1)S(1)} %copy-done.27, f32[512,1152]{1,0:T(8,128)S(1)} %get-tuple-element.75, f32[1152]{0:T(1024)S(1)} %copy-done.47, f32[512,1152]{1,0:T(8,128)S(1)} %copy-done.18, ...), kind=kOutput, calls=%fused_computation.99 | convolution fusion | flops 2729703424 | bytes 21850112 | tf_op jit(solution)/shard_map/tf,df->td/dot_general | solution.py:129
  280.9 13.8 %fusion.141 = f32[8,1024,1024]{2,1,0:T(8,128)} fusion(bf16[1024,8,72]{0,2,1:T(8,128)(2,1)S(1)} %bitcast.149, bf16[1024,8,72]{0,2,1:T(8,128)(2,1)S(1)} %bitcast.144), kind=kOutput, calls=%fused_computation.218 | convolution fusion | flops 1207959552 | bytes 35913728 | tf_op jit(solution)/shard_map/qhd,khd->hqk/dot_general | solution.py:74
  296.3 9.6 %collective-permute-done.7 = bf16[512,1152]{1,0:T(8,128)(2,1)S(1)} collective-permute-done((bf16[512,1152]{1,0:T(8,128)(2,1)S(1)}, bf16[512,1152]{1,0:T(8,128)(2,1)S(1)}, u32[]{:S(2)}, u32[]{:S(2)}) %collective-permute-start.7) | collective-permute-done | bytes 1179680 | tf_op jit(solution)/shard_map/ppermute | solution.py:91
  310.8 19.8 %multiply_convert_fusion = bf16[8,1024,1024]{2,1,0:T(8,128)(2,1)} fusion(f32[8,1024,1024]{2,1,0:T(8,128)} %fusion.141, f32[8,1024]{1,0:T(8,128)S(1)} %bitcast.173, f32[8,1024]{1,0:T(8,128)S(1)} %pad_maximum_fusion.7, bf16[1024,8,72]{0,2,1:T(8,128)(2,1)S(1)} %bitcast.147, bf16[1024,8,72]{0,2,1:T(8,128)(2,1)S(1)} %bitcast.153), kind=kOutput, calls=%fused_computation | convolution fusion | flops 1258291200 | bytes 52756480 | tf_op jit(solution)/shard_map/qhd,khd->hqk/dot_general | solution.py:80
  330.5 8.9 %convolution_convert_fusion.8 = bf16[8,72,1024]{2,1,0:T(8,128)(2,1)S(1)} fusion(bf16[1024,8,72]{0,2,1:T(8,128)(2,1)S(1)} %bitcast.150, bf16[8,1024,1024]{2,1,0:T(8,128)(2,1)} %multiply_convert_fusion), kind=kOutput, calls=%fused_computation.128 | convolution fusion | flops 1208549376 | bytes 19136512 | tf_op jit(solution)/shard_map/hqk,qhd->khd/dot_general | solution.py:86
  339.4 12.2 %convolution_convert_fusion.9 = bf16[8,72,1024]{2,1,0:T(8,128)(2,1)} fusion(bf16[1024,8,72]{0,2,1:T(8,128)(2,1)S(1)} %bitcast.145, bf16[8,1024,1024]{2,1,0:T(8,128)(2,1)} %multiply_convert_fusion), kind=kOutput, calls=%fused_computation.129 | convolution fusion | flops 1208549376 | bytes 19136512 | tf_op jit(solution)/shard_map/hqk,khd->qhd/dot_general | solution.py:85
  351.6 13.4 %fusion.91 = bf16[8,72,1024]{2,1,0:T(8,128)(2,1)S(1)} fusion(bf16[1024,8,72]{0,2,1:T(8,128)(2,1)S(1)} %bitcast.148, f32[8,1024,1024]{2,1,0:T(8,128)} %fusion.141, f32[8,1024]{1,0:T(8,128)} %copy-done.32), kind=kOutput, calls=%fused_computation.127 | convolution fusion | flops 1233715200 | bytes 35946496 | tf_op jit(solution)/shard_map/hqk,qhd->khd/dot_general | solution.py:77
  365.0 8.8 %convolution_convert_fusion.2 = bf16[1152,1728]{0,1:T(8,128)(2,1)S(1)} fusion(bf16[512,1152]{1,0:T(8,128)(2,1)} %copy-done.61, bf16[512,1152]{1,0:T(8,128)(2,1)S(1)} %copy-done.29, bf16[1024,576]{0,1:T(8,128)(2,1)S(1)} %bitcast.154, bf16[1024,576]{0,1:T(8,128)(2,1)S(1)} %bitcast.159, bf16[1024,576]{0,1:T(8,128)(2,1)S(1)} %bitcast.161), kind=kOutput, calls=%fused_computation.15 | convolution fusion | flops 4094189568 | bytes 9879552 | tf_op jit(solution)/shard_map/td,tc->dc/dot_general | solution.py:129
  373.9 2.8 pad_maximum_fusion.1
  378.9 8.6 %copy.30 = bf16[1152,2304]{1,0:T(8,128)(2,1)} copy(bf16[1152,2304]{0,1:T(8,128)(2,1)} %pad_maximum_fusion.1) | data formatting | bytes 10616832
  389.4 6.3 %convolution_convert_fusion.4 = bf16[512,1152]{1,0:T(8,128)(2,1)S(1)} fusion(bf16[1152,2304]{1,0:T(8,128)(2,1)} %all-gather.3.cloned.1.call-done, bf16[1024,1728]{0,1:T(8,128)(2,1)S(1)} %pad_maximum_fusion.2), kind=kOutput, calls=%fused_computation.70 | convolution fusion | flops 2039021568 | bytes 7077888 | tf_op jit(solution)/shard_map/tc,dc->td/dot_general | solution.py:129
  400.9 20.8 %collective-permute-done.8 = bf16[512,1152]{1,0:T(8,128)(2,1)} collective-permute-done((bf16[512,1152]{1,0:T(8,128)(2,1)S(1)}, bf16[512,1152]{1,0:T(8,128)(2,1)}, u32[]{:S(2)}, u32[]{:S(2)}) %collective-permute-start.8) | collective-permute-done | bytes 1179680 | tf_op jit(solution)/shard_map/ppermute | solution.py:91
  421.7 8.4 %fusion.69 = (f32[1152]{0:T(1024)S(1)}, f32[512]{0:T(512)}, f32[512]{0:T(512)}, f32[1152]{0:T(1024)S(1)}, f32[512,1152]{1,0:T(8,128)}) fusion(bf16[1,512,1152]{2,1,0:T(8,128)(2,1)S(1)} %copy-done.4, f32[512]{0:T(512)} %copy-done.54, f32[512]{0:T(512)} %copy-done.50, f32[1152]{0:T(1024)S(1)} %copy-done.41, bf16[512,1152]{1,0:T(8,128)(2,1)} %collective-permute-done.8, ...), kind=kOutput, calls=%fused_computation.96 | convolution fusion | flops 2045506304 | bytes 10638848 | tf_op jit(solution)/shard_map/tc,dc->td/dot_general | solution.py:129
  439.7 4.9 all-to-all-start.2
  445.9 5.4 %all-to-all-done.2 = f32[16,1,432]{2,1,0:T(1,128)} async-done(((f32[16,1,432]{2,1,0:T(1,128)}), f32[16,1,432]{2,1,0:T(1,128)}, u32[]{:S(2)}, u32[]{:S(2)}) %all-to-all-start.2) | async-done | bytes 27680 | tf_op jit(solution)/shard_map/all_to_all | solution.py:262
  451.3 2.9 convolution_bitcast_fusion
  455.9 4.1 all-to-all-start.3
  460.1 3.9 fusion.68
  463.9 2.8 all-to-all-done.3
  469.7 3.8 all-to-all-start.4
  475.9 4.2 all-to-all-done.4
  (239 shorter events, 80.8 us)
Async XLA Ops:
  7.2 21.0 %copy-start = (bf16[1000,576]{0,1:T(8,128)(2,1)S(1)}, bf16[1000,576]{0,1:T(8,128)(2,1)}, u32[]{:S(2)}) copy-start(bf16[1000,576]{0,1:T(8,128)(2,1)} %param.13) | copy-start | bytes 3456004
  7.2 14.6 %copy-start.2 = (bf16[1,512,1152]{2,1,0:T(8,128)(2,1)S(1)}, bf16[1,512,1152]{2,1,0:T(8,128)(2,1)}, u32[]{:S(2)}) copy-start(bf16[1,512,1152]{2,1,0:T(8,128)(2,1)} %param.10) | copy-start | bytes 3538948
  7.2 68.2 %all-gather.3.cloned.1.call-start = ((), (), s32[]{:S(2)}) async-start(), calls=%async_computation.7 | async-start | bytes 5640192 | tf_op jit(solution)/shard_map/all_gather | solution.py:150
  10.2 18.4 %copy-start.21 = (bf16[576,432]{0,1:T(8,128)(2,1)S(1)}, bf16[576,432]{0,1:T(8,128)(2,1)}, u32[]{:S(2)}) copy-start(bf16[576,432]{0,1:T(8,128)(2,1)} %param.14) | copy-start | bytes 1492996
  10.2 149.5 %all-gather.5.cloned.1.call-start = ((), (), s32[]{:S(2)}) async-start(), calls=%async_computation.8 | async-start | bytes 11280384 | tf_op jit(solution)/shard_map/all_gather | solution.py:156
  14.3 13.8 %all-to-all-start = ((s32[16,1,2]{2,1,0:T(1,128)}), s32[16,1,2]{2,1,0:T(1,128)S(1)}, u32[]{:S(2)}, u32[]{:S(2)}) async-start(s32[16,1,2]{2,1,0:T(1,128)} %tile.4), calls=%async_computation | async-start | bytes 16384 | tf_op jit(solution)/shard_map/all_to_all | solution.py:117
  22.0 23.4 %copy-start.50 = (f32[512]{0:T(512)}, f32[512]{0:T(512)S(1)}, u32[]{:S(2)}) copy-start(f32[512]{0:T(512)S(1)} %broadcast_multiply_fusion.5) | copy-start | bytes 6148
  28.2 16.7 %copy-start.58 = (s32[16]{0:T(128)}, s32[16]{0:T(128)S(1)}, u32[]{:S(2)}) copy-start(s32[16]{0:T(128)S(1)} %get-tuple-element.93) | copy-start | bytes 196
  28.7 18.3 %copy-start.26 = (bf16[1,512,1152]{2,1,0:T(8,128)(2,1)S(1)}, bf16[1,512,1152]{2,1,0:T(8,128)(2,1)}, u32[]{:S(2)}) copy-start(bf16[1,512,1152]{2,1,0:T(8,128)(2,1)} %param.19) | copy-start | bytes 3538948
  29.3 3.9 collective-permute-start
  33.8 10.2 %all-to-all-start.1 = ((f32[16,1,432]{2,1,0:T(1,128)}), f32[16,1,432]{2,1,0:T(1,128)S(1)}, u32[]{:S(2)}, u32[]{:S(2)}) async-start(f32[16,1,432]{2,1,0:T(1,128)} %copy.25), calls=%async_computation.1 | async-start | bytes 65536 | tf_op jit(solution)/shard_map/all_to_all | solution.py:167
  37.3 339.3 %reduce-scatter.5.cloned.1.call-start = ((), (), s32[]{:S(2)}) async-start(), calls=%async_computation.9 | async-start | bytes 11280384 | tf_op jit(solution)/shard_map/reduce_scatter | solution.py:216
  45.4 35.3 %copy-start.28 = (bf16[512,1152]{1,0:T(8,128)(2,1)}, bf16[512,1152]{1,0:T(8,128)(2,1)S(1)}, u32[]{:S(2)}) copy-start(bf16[512,1152]{1,0:T(8,128)(2,1)S(1)} %fusion.63) | copy-start | bytes 3538948
  45.4 27.5 %collective-permute-start.1 = (bf16[512,1152]{1,0:T(8,128)(2,1)S(1)}, bf16[512,1152]{1,0:T(8,128)(2,1)S(1)}, u32[]{:S(2)}, u32[]{:S(2)}) collective-permute-start(bf16[512,1152]{1,0:T(8,128)(2,1)S(1)} %fusion.63), channel_id=1, source_target_pairs={{0,1},{1,0},{2,3},{3,2},{4,5},{5,4},{6,7},{7,6},{8,9},{9,8},{10,11... | collective-permute-start | bytes 3538952 | tf_op jit(solution)/shard_map/ppermute | solution.py:91
  47.2 33.4 %copy-start.30 = (bf16[512,1152]{1,0:T(8,128)(2,1)}, bf16[512,1152]{1,0:T(8,128)(2,1)S(1)}, u32[]{:S(2)}) copy-start(bf16[512,1152]{1,0:T(8,128)(2,1)S(1)} %fusion.71) | copy-start | bytes 3538948
  74.0 26.7 %collective-permute-start.2 = (bf16[512,1152]{1,0:T(8,128)(2,1)S(1)}, bf16[512,1152]{1,0:T(8,128)(2,1)}, u32[]{:S(2)}, u32[]{:S(2)}) collective-permute-start(bf16[512,1152]{1,0:T(8,128)(2,1)S(1)} %fusion.71), channel_id=1, source_target_pairs={{0,1},{1,0},{2,3},{3,2},{4,5},{5,4},{6,7},{7,6},{8,9},{9,8},{10,11... | collective-permute-start | bytes 3538952 | tf_op jit(solution)/shard_map/ppermute | solution.py:91
  86.9 21.3 %copy-start.6 = (bf16[1024,576]{0,1:T(8,128)(2,1)}, bf16[1024,576]{0,1:T(8,128)(2,1)S(1)}, u32[]{:S(2)}) copy-start(bf16[1024,576]{0,1:T(8,128)(2,1)S(1)} %get-tuple-element.77) | copy-start | bytes 3538948
  100.7 25.8 %collective-permute-start.3 = (bf16[512,1152]{1,0:T(8,128)(2,1)S(1)}, bf16[512,1152]{1,0:T(8,128)(2,1)S(1)}, u32[]{:S(2)}, u32[]{:S(2)}) collective-permute-start(bf16[512,1152]{1,0:T(8,128)(2,1)S(1)} %convolution_convert_fusion.5), channel_id=1, source_target_pairs={{0,1},{1,0},{2,3},{3,2},{4,5},{5,4},{6,7},{7,6},{8,9},{9,8},{10,11... | collective-permute-start | bytes 3538952 | tf_op jit(solution)/shard_map/ppermute | solution.py:91
  108.3 18.2 %copy-start.3 = (bf16[1,512,1152]{2,1,0:T(8,128)(2,1)S(1)}, bf16[1,512,1152]{2,1,0:T(8,128)(2,1)}, u32[]{:S(2)}) copy-start(bf16[1,512,1152]{2,1,0:T(8,128)(2,1)} %param.10) | copy-start | bytes 3538948
  108.3 18.2 %copy-start.42 = (f32[1152]{0:T(1024)S(1)}, f32[1152]{0:T(1024)}, u32[]{:S(2)}) copy-start(f32[1152]{0:T(1024)} %get-tuple-element.71) | copy-start | bytes 13828
  112.2 19.2 %copy-start.11 = (bf16[8,72,512]{2,1,0:T(8,128)(2,1)}, bf16[8,72,512]{2,1,0:T(8,128)(2,1)S(1)}, u32[]{:S(2)}) copy-start(bf16[8,72,512]{2,1,0:T(8,128)(2,1)S(1)} %fusion.95) | copy-start | bytes 1769476
  133.6 38.4 %collective-permute-start.4 = (bf16[512,1152]{1,0:T(8,128)(2,1)}, bf16[512,1152]{1,0:T(8,128)(2,1)}, u32[]{:S(2)}, u32[]{:S(2)}) collective-permute-start(bf16[512,1152]{1,0:T(8,128)(2,1)} %add_convert_fusion.1), channel_id=1, source_target_pairs={{0,1},{1,0},{2,3},{3,2},{4,5},{5,4},{6,7},{7,6},{8,9},{9,8},{10,11... | collective-permute-start | bytes 3538952 | tf_op jit(solution)/shard_map/ppermute | solution.py:91
  166.6 32.8 %copy-start.63 = (bf16[512,2304]{1,0:T(8,128)(2,1)}, bf16[512,2304]{1,0:T(8,128)(2,1)S(1)}, u32[]{:S(2)}) copy-start(bf16[512,2304]{1,0:T(8,128)(2,1)S(1)} %get-tuple-element.24) | copy-start | bytes 7077892
  172.0 18.0 %copy-start.62 = (bf16[512,2304]{1,0:T(8,128)(2,1)}, bf16[512,2304]{1,0:T(8,128)(2,1)S(1)}, u32[]{:S(2)}) copy-start(bf16[512,2304]{1,0:T(8,128)(2,1)S(1)} %fusion.21) | copy-start | bytes 7077892
  178.0 21.4 %copy-start.64 = (bf16[512,2304]{1,0:T(8,128)(2,1)}, bf16[512,2304]{1,0:T(8,128)(2,1)S(1)}, u32[]{:S(2)}) copy-start(bf16[512,2304]{1,0:T(8,128)(2,1)S(1)} %get-tuple-element.27) | copy-start | bytes 7077892
  197.8 28.5 %collective-permute-start.6 = (bf16[512,1152]{1,0:T(8,128)(2,1)}, bf16[512,1152]{1,0:T(8,128)(2,1)}, u32[]{:S(2)}, u32[]{:S(2)}) collective-permute-start(bf16[512,1152]{1,0:T(8,128)(2,1)} %fusion.43), channel_id=1, source_target_pairs={{0,1},{1,0},{2,3},{3,2},{4,5},{5,4},{6,7},{7,6},{8,9},{9,8},{10,11... | collective-permute-start | bytes 3538952 | tf_op jit(solution)/shard_map/ppermute | solution.py:91
  234.5 250.4 %reduce-scatter.7.cloned.1.call-start = ((), (), s32[]{:S(2)}) async-start(), calls=%async_computation.10 | async-start | bytes 5640192
  241.2 27.3 %collective-permute-start.5 = (bf16[512,1152]{1,0:T(8,128)(2,1)S(1)}, bf16[512,1152]{1,0:T(8,128)(2,1)S(1)}, u32[]{:S(2)}, u32[]{:S(2)}) collective-permute-start(bf16[512,1152]{1,0:T(8,128)(2,1)S(1)} %fusion.46), channel_id=1, source_target_pairs={{0,1},{1,0},{2,3},{3,2},{4,5},{5,4},{6,7},{7,6},{8,9},{9,8},{10,11... | collective-permute-start | bytes 3538952 | tf_op jit(solution)/shard_map/ppermute | solution.py:91
  242.8 68.0 %copy-start.32 = (f32[8,1024]{1,0:T(8,128)}, f32[8,1024]{1,0:T(8,128)S(1)}, u32[]{:S(2)}) copy-start(f32[8,1024]{1,0:T(8,128)S(1)} %pad_maximum_fusion.7) | copy-start | bytes 98308
  242.8 25.7 %copy-start.18 = (f32[512,1152]{1,0:T(8,128)S(1)}, f32[512,1152]{1,0:T(8,128)}, u32[]{:S(2)}) copy-start(f32[512,1152]{1,0:T(8,128)} %get-tuple-element.98) | copy-start | bytes 7077892
  242.8 25.7 %copy-start.25 = (bf16[512,1152]{1,0:T(8,128)(2,1)S(1)}, bf16[512,1152]{1,0:T(8,128)(2,1)}, u32[]{:S(2)}) copy-start(bf16[512,1152]{1,0:T(8,128)(2,1)} %copy-done.24) | copy-start | bytes 3538948
  242.8 25.7 %copy-start.27 = (bf16[1,512,1152]{2,1,0:T(8,128)(2,1)S(1)}, bf16[1,512,1152]{2,1,0:T(8,128)(2,1)}, u32[]{:S(2)}) copy-start(bf16[1,512,1152]{2,1,0:T(8,128)(2,1)} %param.19) | copy-start | bytes 3538948
  242.9 25.7 %copy-start.47 = (f32[1152]{0:T(1024)S(1)}, f32[1152]{0:T(1024)}, u32[]{:S(2)}) copy-start(f32[1152]{0:T(1024)} %copy-done.46) | copy-start | bytes 13828
  268.6 26.1 %slice-start.1 = ((s8[5308416]{0:T(1024)(128)(4,1)}), s8[4194304]{0:T(1024)(128)(4,1)S(1)}, s32[]{:S(2)}) async-start(s8[5308416]{0:T(1024)(128)(4,1)} %bitcast.169), calls=%async_computation.12 | async-start | bytes 8388608
  279.4 26.5 %collective-permute-start.7 = (bf16[512,1152]{1,0:T(8,128)(2,1)S(1)}, bf16[512,1152]{1,0:T(8,128)(2,1)S(1)}, u32[]{:S(2)}, u32[]{:S(2)}) collective-permute-start(bf16[512,1152]{1,0:T(8,128)(2,1)S(1)} %multiply_convert_fusion.3), channel_id=1, source_target_pairs={{0,1},{1,0},{2,3},{3,2},{4,5},{5,4},{6,7},{7,6},{8,9},{9,8},{10,11... | collective-permute-start | bytes 3538952 | tf_op jit(solution)/shard_map/ppermute | solution.py:91
  395.7 25.9 %copy-start.4 = (bf16[1,512,1152]{2,1,0:T(8,128)(2,1)S(1)}, bf16[1,512,1152]{2,1,0:T(8,128)(2,1)}, u32[]{:S(2)}) copy-start(bf16[1,512,1152]{2,1,0:T(8,128)(2,1)} %param.10) | copy-start | bytes 3538948
  395.7 25.9 %copy-start.41 = (f32[1152]{0:T(1024)S(1)}, f32[1152]{0:T(1024)}, u32[]{:S(2)}) copy-start(f32[1152]{0:T(1024)} %copy-done.40) | copy-start | bytes 13828
  395.8 25.9 %collective-permute-start.8 = (bf16[512,1152]{1,0:T(8,128)(2,1)S(1)}, bf16[512,1152]{1,0:T(8,128)(2,1)}, u32[]{:S(2)}, u32[]{:S(2)}) collective-permute-start(bf16[512,1152]{1,0:T(8,128)(2,1)S(1)} %convolution_convert_fusion.4), channel_id=1, source_target_pairs={{0,1},{1,0},{2,3},{3,2},{4,5},{5,4},{6,7},{7,6},{8,9},{9,8},{10,11... | collective-permute-start | bytes 3538952 | tf_op jit(solution)/shard_map/ppermute | solution.py:91
  400.9 59.2 %copy-start.51 = (f32[512]{0:T(512)S(1)}, f32[512]{0:T(512)}, u32[]{:S(2)}) copy-start(f32[512]{0:T(512)} %copy-done.50) | copy-start | bytes 6148
  400.9 59.2 %copy-start.55 = (f32[512]{0:T(512)S(1)}, f32[512]{0:T(512)}, u32[]{:S(2)}) copy-start(f32[512]{0:T(512)} %copy-done.54) | copy-start | bytes 6148
  421.7 38.4 %copy-start.9 = (f32[512,1152]{1,0:T(8,128)S(1)}, f32[512,1152]{1,0:T(8,128)}, u32[]{:S(2)}) copy-start(f32[512,1152]{1,0:T(8,128)} %copy-done.8) | copy-start | bytes 7077892
  434.2 4.1 collective-permute-start.9
  439.7 11.6 %all-to-all-start.2 = ((f32[16,1,432]{2,1,0:T(1,128)}), f32[16,1,432]{2,1,0:T(1,128)}, u32[]{:S(2)}, u32[]{:S(2)}) async-start(f32[16,1,432]{2,1,0:T(1,128)} %all_to_all.31), calls=%async_computation.2 | async-start | bytes 65536 | tf_op jit(solution)/shard_map/all_to_all | solution.py:262
  455.9 10.9 %all-to-all-start.3 = ((f32[16,1,576]{2,1,0:T(1,128)}), f32[16,1,576]{2,1,0:T(1,128)}, u32[]{:S(2)}, u32[]{:S(2)}) async-start(f32[16,1,576]{2,1,0:T(1,128)} %reshape.184), calls=%async_computation.3 | async-start | bytes 81920 | tf_op jit(solution)/shard_map/all_to_all | solution.py:123
  463.9 17.2 %copy-start.34 = (f32[16,576]{1,0:T(8,128)S(1)}, f32[16,576]{1,0:T(8,128)}, u32[]{:S(2)}) copy-start(f32[16,576]{1,0:T(8,128)} %copy-done.33) | copy-start | bytes 110596
  463.9 17.2 %copy-start.59 = (s32[16]{0:T(128)S(1)}, s32[16]{0:T(128)}, u32[]{:S(2)}) copy-start(s32[16]{0:T(128)} %copy-done.58) | copy-start | bytes 196
  468.9 14.8 %copy-start.10 = (f32[72,4608]{1,0:T(8,128)S(1)}, f32[72,4608]{1,0:T(8,128)}, u32[]{:S(2)}) copy-start(f32[72,4608]{1,0:T(8,128)} %convert_element_type.207) | copy-start | bytes 3981316
  469.7 10.4 %all-to-all-start.4 = ((f32[16,1,576]{2,1,0:T(1,128)}), f32[16,1,576]{2,1,0:T(1,128)S(1)}, u32[]{:S(2)}, u32[]{:S(2)}) async-start(f32[16,1,576]{2,1,0:T(1,128)} %reshape.186), calls=%async_computation.4 | async-start | bytes 81920 | tf_op jit(solution)/shard_map/all_to_all | solution.py:117
  (39 other events, 225.2 us)
Sparse Core Ops, SparseCore 0:
  10.7 59.0 all-gather.2
  72.7 86.9 all-gather.4
  234.6 118.9 reduce-scatter.4
  387.6 77.4 reduce-scatter.6
